TPU v7x, 256 devices: a whole 4x4x8 slice. The times are simulated.
256 devices in a mesh: ox: 16 (over y, z_lo, core), oy: 16 (over z_hi, x).
Axes of the slice: x: 4, y: 4, z: 8 (z_hi: 4, z_lo: 2; z = z_hi * 2 + z_lo), core: 2. Of those that a mesh axis runs over, the one named last changes fastest.
Arguments:
- slip_rate: bfloat16 [4, 8192], P(None, ('ox', 'oy')), may hold values from -6 to 6
- green_kernel: bfloat16 [8192, 9, 8192], P(('ox', 'oy')), may hold values from -1 to 1
- intersection: int32 [256, 9], P(('ox', 'oy')), may hold values 0 or 1
- wet_mask: int32 [4096, 8192], P('ox', 'oy'), may hold values 0 or 1
- column_height: float32 [4096, 8192], P('ox', 'oy'), may hold values from 3 to 5
- east_flow: float32 [4096, 8192], P('ox', 'oy'), may hold values from -3 to 3
- north_flow: float32 [4096, 8192], P('ox', 'oy'), may hold values from -3 to 3
Outputs:
- height_out: float32 [4096, 8192], P('ox', 'oy')
- east_out: float32 [4096, 8192], P('ox', 'oy')
- north_out: float32 [4096, 8192], P('ox', 'oy')
All inputs are finite; a program needn't handle non-finite values. No bound on the sum of `intersection` or of `wet_mask` on one device may be relied on, other than what follows from the above.
Results may differ from a plain program's by a relative error of at most 0.0003.
Values sent between devices are 32-bit elements; how exact they have to be, the bound alone decides.
No kernel may reach another device: no remote copies, remote signals or barrier semaphores. Data moves between devices by JAX's collectives and lax.ppermute only.
A program may use at most 64 MiB of HBM per device.

v0:
```python
import functools

import jax
import jax.numpy as jnp
from jax import lax
from jax.experimental import pallas as pl
from jax.experimental.pallas import tpu as pltpu
from jax.sharding import PartitionSpec as P

STEPS = 4
SIDE = 16
ROWS = 256
COLS = 512
LANES = 128
UX = 64
EXT = ROWS + 8
WIDE = COLS + LANES
MAIN = STEPS * UX
RING = MAIN + 8
SLIVER = 3 * MAIN
EDGE = SLIVER + 16
ROW_MSG = EDGE + 64
TURNED = RING
COL_MSG = RING + 48
VMEM_LIMIT = 48 * 1024 * 1024
UNROLL = 4


def partners(axis, parity, reach):
    return [
        (i, (i + reach if (i // reach) % 2 == parity else i - reach) % SIDE)
        for i in range(SIDE)
    ]


def swap(value, axis, parity, reach=1):
    return lax.ppermute(value, axis, partners(axis, parity, reach))


def slip_kernel(
    place, cover_in, slip_in, green, h_in, m_in, n_in, w_in,
    msg_a, msg_b, far_a, far_b, own, held, cover, slip, edge_f, edge_i, sems,
):
    def fetch(slot):
        return pltpu.make_async_copy(green.at[slot], held.at[slot], sems.at[slot])

    small = [
        pltpu.make_async_copy(slip_in, slip, sems.at[9]),
        pltpu.make_async_copy(cover_in, cover, sems.at[10]),
    ]
    edges = []
    for f, field in enumerate((h_in, m_in, n_in, w_in)):
        for t, start in enumerate((0, ROWS - 8)):
            target = edge_f.at[f, t] if f < 3 else edge_i.at[t]
            edges.append(
                pltpu.make_async_copy(field.at[start : start + 8], target, sems.at[11 + 2 * f + t])
            )
    for copy in small:
        copy.start()
    order = (0, 6, 3, 1, 7, 4, 2, 8, 5)
    for slot in order:
        fetch(slot).start()
    for copy in edges:
        copy.start()
    for copy in small:
        copy.wait()
    even = place[0] % 2 == 0
    even2 = (place[0] // 2) % 2 == 0

    rates = slip[...].astype(jnp.float32)
    rates = jnp.concatenate([rates] * 8, axis=1)
    rates = jnp.concatenate(
        [jnp.broadcast_to(rates[s : s + 1], (8, 256)) for s in range(STEPS)], axis=0
    )
    row = lax.broadcasted_iota(jnp.int32, (32, 256), 0)
    col = lax.broadcasted_iota(jnp.int32, (32, 256), 1)
    spread = jnp.where(col // 32 == row % 8, rates, 0.0).astype(jnp.bfloat16)

    def group(slot, g):
        right = jnp.concatenate(
            [held[slot, :, (g * 8 + p) * LANES : (g * 8 + p + 1) * LANES] for p in range(8)],
            axis=0,
        )
        value = jnp.dot(spread, right, preferred_element_type=jnp.float32)
        return value * cover[0, slot].astype(jnp.float32)

    for b in range(3):
        fetch(b).wait()
        fetch(6 + b).wait()
        fetch(3 + b).wait()
        for g in range(8):
            up = group(b, g)
            down = group(6 + b, g)
            mid = group(3 + b, g)
            first = jnp.where(even, down, up)
            second = jnp.where(even, up, down)
            for s in range(STEPS):
                part = slice(8 * s, 8 * s + 8)
                at = s * UX + g * 8
                msg_a[b * MAIN + at : b * MAIN + at + 8, :] = first[part]
                msg_b[b * MAIN + at : b * MAIN + at + 8, :] = second[part]
                own[b, at : at + 8, :] = mid[part]
            if g == 0:
                for s in range(STEPS):
                    own[b, MAIN + s : MAIN + s + 1, :] = down[8 * s : 8 * s + 1]
                up_edge, up_mid = up, mid
            if g == 7:
                for s in range(STEPS):
                    own[b, MAIN + 4 + s : MAIN + 5 + s, :] = up[8 * s + 7 : 8 * s + 8]
                    at = b * STEPS + s
                    to_down = mid[8 * s + 7 : 8 * s + 8]
                    to_up = up_mid[8 * s : 8 * s + 1]
                    msg_a[SLIVER + at : SLIVER + at + 1, :] = jnp.where(even, to_down, to_up)
                    msg_b[SLIVER + at : SLIVER + at + 1, :] = jnp.where(even, to_up, to_down)
                    to_down = down[8 * s + 7 : 8 * s + 8]
                    to_up = up_edge[8 * s : 8 * s + 1]
                    far_a[at : at + 1, :] = jnp.where(even2, to_down, to_up)
                    far_b[at : at + 1, :] = jnp.where(even2, to_up, to_down)
    blank = jnp.zeros((4, LANES), jnp.float32)
    for ref, start in ((msg_a, SLIVER), (msg_b, SLIVER), (far_a, 0), (far_b, 0)):
        ref[start + 12 : start + 16, :] = blank

    for copy in edges:
        copy.wait()
    for f in range(4):
        top, bottom = (edge_f[f, 0], edge_f[f, 1]) if f < 3 else (edge_i[0], edge_i[1])
        to_up = top[0:4].astype(jnp.float32)
        to_down = bottom[4:8].astype(jnp.float32)
        first = jnp.where(even, to_down, to_up)
        second = jnp.where(even, to_up, to_down)
        for k in range(4):
            at = EDGE + (f * 4 + k) * 4
            msg_a[at : at + 4, :] = first[:, k * LANES : (k + 1) * LANES]
            msg_b[at : at + 4, :] = second[:, k * LANES : (k + 1) * LANES]


def column_kernel(
    place, own, got_a, got_b, gotfar_a, gotfar_b, h_l, h_r, m_l, m_r, n_l, n_r, w_l, w_r,
    msg_a, msg_b, far_a, far_b, centre, ring, edges, lanes,
):
    i, j = place[0], place[1]
    even = i % 2 == 0
    even2 = (i // 2) % 2 == 0
    above_ok, below_ok = i > 0, i < SIDE - 1
    above2_ok, below2_ok = i > 1, i < SIDE - 2
    even_j = j % 2 == 0
    even2_j = (j // 2) % 2 == 0

    lane = lax.broadcasted_iota(jnp.int32, (EXT, LANES), 1)

    def from_above(rows):
        return jnp.where(even, got_b[rows, :], got_a[rows, :])

    def from_below(rows):
        return jnp.where(even, got_a[rows, :], got_b[rows, :])

    sums = []
    for b in range(3):
        rows = slice(b * MAIN, (b + 1) * MAIN)
        main = own[b, 0:MAIN, :]
        main = main + jnp.where(above_ok, from_above(rows), 0.0)
        main = main + jnp.where(below_ok, from_below(rows), 0.0)
        rows = slice(SLIVER + 4 * b, SLIVER + 4 * b + 4)
        far = slice(4 * b, 4 * b + 4)
        above = jnp.where(above_ok, from_above(rows), 0.0)
        above = above + jnp.where(
            above2_ok, jnp.where(even2, gotfar_b[far, :], gotfar_a[far, :]), 0.0
        )
        below = jnp.where(below_ok, from_below(rows), 0.0)
        below = below + jnp.where(
            below2_ok, jnp.where(even2, gotfar_a[far, :], gotfar_b[far, :]), 0.0
        )
        tail = own[b, MAIN:RING, :] + jnp.concatenate([below, above], axis=0)
        sums.append(jnp.concatenate([main, tail], axis=0))
    left_sum, mid_sum, right_sum = sums

    msg_a[0:RING, :] = jnp.where(even_j, right_sum, left_sum)
    msg_b[0:RING, :] = jnp.where(even_j, left_sum, right_sum)
    centre[...] = mid_sum

    for f in range(4):
        for k in range(4):
            rows = slice(EDGE + (f * 4 + k) * 4, EDGE + (f * 4 + k) * 4 + 4)
            edges[f, :, k * LANES : (k + 1) * LANES] = jnp.concatenate(
                [from_below(rows), from_above(rows)], axis=0
            )

    packed = jnp.zeros((EXT, LANES), jnp.float32)

    def place_lanes(packed, block, source, target, count):
        moved = pltpu.roll(block, (target - source) % LANES, 1) if target != source else block
        return jnp.where((lane >= target) & (lane < target + count), moved, packed)

    fields = ((h_l, h_r), (m_l, m_r), (n_l, n_r), (w_l, w_r))
    for f, (left, right) in enumerate(fields):
        lo = jnp.concatenate([left[...].astype(jnp.float32), edges[f, :, 0:LANES]], axis=0)
        hi = jnp.concatenate(
            [right[...].astype(jnp.float32), edges[f, :, COLS - LANES : COLS]], axis=0
        )
        packed = place_lanes(packed, hi, LANES - 4, 4 * f, 4)
        packed = place_lanes(packed, lo, 0, 16 + 4 * f, 4)
    packed = place_lanes(packed, mid_sum, LANES - 1, 12, 1)
    packed = place_lanes(packed, mid_sum, 0, 31, 1)
    packed = place_lanes(packed, right_sum, LANES - 1, 32, 1)
    packed = place_lanes(packed, left_sum, 0, 33, 1)
    packed = place_lanes(packed, left_sum, LANES - 1, 34, 1)
    packed = place_lanes(packed, right_sum, 0, 35, 1)
    lanes[0:EXT, :] = packed
    lanes[EXT:384, :] = jnp.zeros((384 - EXT, LANES), jnp.float32)

    zero8 = jnp.zeros((8, LANES), jnp.float32)
    far_a[...] = zero8
    far_b[...] = zero8
    ring[...] = zero8
    for k in range(3):
        turned = lanes[k * LANES : (k + 1) * LANES, :].T
        at = TURNED + 16 * k
        msg_a[at : at + 16, :] = jnp.where(even_j, turned[0:16], turned[16:32])
        msg_b[at : at + 16, :] = jnp.where(even_j, turned[16:32], turned[0:16])
        far_a[k : k + 1, :] = jnp.where(even2_j, turned[32:33], turned[33:34])
        far_b[k : k + 1, :] = jnp.where(even2_j, turned[33:34], turned[32:33])
        ring[k : k + 1, :] = turned[34:35]
        ring[4 + k : 5 + k, :] = turned[35:36]


def step_kernel(
    place, centre, got_a, got_b, gotfar_a, gotfar_b, ring, edges, h_in, m_in, n_in, w_in,
    h_out, m_out, n_out, state_a, state_b, wet, lift, turned,
):
    i, j = place[0], place[1]
    even_j = j % 2 == 0
    even2_j = (j // 2) % 2 == 0
    top, bottom = i == 0, i == SIDE - 1
    left_end, right_end = j == 0, j == SIDE - 1

    def from_left(rows):
        return jnp.where(even_j, got_b[rows, :], got_a[rows, :])

    def from_right(rows):
        return jnp.where(even_j, got_a[rows, :], got_b[rows, :])

    rows = slice(0, RING)
    total = centre[...] + jnp.where(left_end, 0.0, from_left(rows))
    total = 0.05 * (total + jnp.where(right_end, 0.0, from_right(rows)))
    coarse = lax.broadcasted_iota(jnp.int32, (LANES, COLS), 0)
    fine = lax.broadcasted_iota(jnp.int32, (LANES, COLS), 1)
    spread = jnp.where(fine // 4 == coarse, 1.0, 0.0).astype(jnp.bfloat16)
    part = total.astype(jnp.bfloat16)
    rest = total - part.astype(jnp.float32)
    part2 = rest.astype(jnp.bfloat16)
    part3 = (rest - part2.astype(jnp.float32)).astype(jnp.bfloat16)
    dot = functools.partial(jnp.dot, preferred_element_type=jnp.float32)
    lift[:, 0:COLS] = dot(part, spread) + dot(part2, spread) + dot(part3, spread)

    turned[40:LANES, :] = jnp.zeros((LANES - 40, LANES), jnp.float32)
    beside = []
    for k in range(3):
        at = TURNED + 16 * k
        left = from_left(slice(at, at + 16))
        right = from_right(slice(at, at + 16))
        for f in range(4):
            turned[8 * f : 8 * f + 4, :] = left[4 * f : 4 * f + 4]
            turned[8 * f + 4 : 8 * f + 8, :] = right[4 * f : 4 * f + 4]
        far_left = jnp.where(even2_j, gotfar_b[k : k + 1, :], gotfar_a[k : k + 1, :])
        far_right = jnp.where(even2_j, gotfar_a[k : k + 1, :], gotfar_b[k : k + 1, :])
        ring_left = ring[k : k + 1, :] + left[12:13] + jnp.where(j > 1, far_left, 0.0)
        ring_right = ring[4 + k : 5 + k, :] + right[15:16]
        ring_right = ring_right + jnp.where(j < SIDE - 2, far_right, 0.0)
        turned[32:36, :] = jnp.broadcast_to(0.05 * ring_left, (4, LANES))
        turned[36:40, :] = jnp.broadcast_to(0.05 * ring_right, (4, LANES))
        beside.append(turned[...].T)
    beside = jnp.concatenate([beside[0], beside[1], beside[2][0:8]], axis=0)

    def side_block(f):
        return pltpu.roll(beside, (LANES - 4 - 8 * f) % LANES, 1)

    for f, field in enumerate((h_in, m_in, n_in)):
        state_a[f, 0:ROWS, 0:COLS] = field[...]
        state_a[f, ROWS:EXT, 0:COLS] = edges[f]
        state_a[f, :, COLS:WIDE] = side_block(f)
    wet[0:ROWS, 0:COLS] = w_in[...].astype(jnp.float32)
    wet[ROWS:EXT, 0:COLS] = edges[3]
    wet[:, COLS:WIDE] = side_block(3)
    lift[:, COLS:WIDE] = side_block(4)

    sub = lax.broadcasted_iota(jnp.int32, (8, WIDE), 0)
    first_row, last_row, upper_half = sub == 0, sub == 7, sub < 4
    lane = lax.broadcasted_iota(jnp.int32, (8, LANES), 1)
    lane_left = (lane == LANES - 1) & left_end
    lane_right = (lane == 0) & right_end

    def load(ref, f, at):
        value = ref[f, pl.ds(at, 8), :]
        block = value[:, COLS:WIDE]
        block = jnp.where(lane_left, pltpu.roll(value[:, 0:LANES], LANES - 1, 1), block)
        block = jnp.where(lane_right, pltpu.roll(value[:, COLS - LANES : COLS], 1, 1), block)
        return jnp.concatenate([value[:, 0:COLS], block], axis=1)

    def fluxes(ref, at):
        height, east, north = load(ref, 0, at), load(ref, 1, at), load(ref, 2, at)
        inverse = 1.0 / height
        v = north * inverse
        pressure = 0.05 * height * height
        fm = 0.1 * east
        gn = 0.1 * north
        fmm = fm * (east * inverse) + pressure
        fmn = fm * v
        gnn = gn * v + pressure
        quarter = (0.25 * height, 0.25 * east, 0.25 * north)
        return quarter, (fm, fmm, fmn), (gn, fmn, gnn)

    def down_shift(quarter, flux):
        return [pltpu.roll(q + x, 1, 0) for q, x in zip(quarter, flux)]

    def up_shift(quarter, flux):
        return [pltpu.roll(q - x, 7, 0) for q, x in zip(quarter, flux)]

    def across(quarter, flux):
        return [
            pltpu.roll(q - x, WIDE - 1, 1) + pltpu.roll(q + x, 1, 1)
            for q, x in zip(quarter, flux)
        ]

    zeros = jnp.zeros((8, WIDE), jnp.float32)

    for s in range(STEPS):
        source, target = (state_a, state_b) if s % 2 == 0 else (state_b, state_a)
        final = s == STEPS - 1
        for f in range(3):
            source[f, EXT - 1 : EXT, :] = jnp.where(
                top, source[f, 0:1, :], source[f, EXT - 1 : EXT, :]
            )
            source[f, ROWS : ROWS + 1, :] = jnp.where(
                bottom, source[f, ROWS - 1 : ROWS, :], source[f, ROWS : ROWS + 1, :]
            )

        def visit(at, above, source=source):
            quarter, east_flux, north_flux = fluxes(source, at)
            below = down_shift(quarter, east_flux)
            ahead = up_shift(quarter, east_flux)
            partial = [
                w + jnp.where(first_row, a, b) + jnp.where(last_row, 0.0, u)
                for w, a, b, u in zip(across(quarter, north_flux), above, below, ahead)
            ]
            return partial, below, ahead

        def finish(at, upper, lower, partial, ahead, s=s, final=final, target=target):
            height, east, north = [
                p + jnp.where(last_row, u, 0.0) for p, u in zip(partial, ahead)
            ]
            raised = jnp.where(
                upper_half,
                jnp.broadcast_to(lift[pl.ds(upper, 1), :], (8, WIDE)),
                jnp.broadcast_to(lift[pl.ds(lower, 1), :], (8, WIDE)),
            )
            height = height + raised
            mask = wet[pl.ds(at, 8), :]
            east = east * mask
            north = north * mask
            if final:
                h_out[pl.ds(at, 8), :] = height[:, 0:COLS]
                m_out[pl.ds(at, 8), :] = east[:, 0:COLS]
                n_out[pl.ds(at, 8), :] = north[:, 0:COLS]
            else:
                target[0, pl.ds(at, 8), :] = height
                target[1, pl.ds(at, 8), :] = east
                target[2, pl.ds(at, 8), :] = north

        quarter, east_flux, _ = fluxes(source, ROWS)
        above = down_shift(quarter, east_flux)
        partial, above, _ = visit(0, above)

        def body(c, carry, visit=visit, finish=finish, s=s):
            partial, above = carry
            at = pl.multiple_of(c * 8, 8)
            new_partial, new_above, ahead = visit(at, above)
            before = pl.multiple_of(at - 8, 8)
            row = s * UX + 2 * (c - 1)
            finish(before, row, row + 1, partial, ahead)
            return new_partial, new_above

        partial, above = lax.fori_loop(1, EXT // 8, body, (partial, above), unroll=UNROLL)
        if not final:
            quarter, east_flux, _ = fluxes(source, 0)
            ahead = up_shift(quarter, east_flux)
            finish(ROWS, MAIN + s, MAIN + 4 + s, partial, ahead)


def whole(shape):
    return pl.BlockSpec(shape, lambda g: (0,) * len(shape))


def smem():
    return pl.BlockSpec(memory_space=pltpu.SMEM)


def f32(*shape):
    return jax.ShapeDtypeStruct(shape, jnp.float32)


def run(body, outs, in_specs, scratch, args, name):
    return pl.pallas_call(
        body,
        grid=(1,),
        in_specs=in_specs,
        out_specs=[whole(o.shape) for o in outs],
        out_shape=outs,
        scratch_shapes=scratch,
        compiler_params=pltpu.CompilerParams(vmem_limit_bytes=VMEM_LIMIT),
        name=name,
    )(*args)


def shards(slip_rate, green_kernel, intersection, wet_mask, column_height, east_flow, north_flow):
    place = jnp.stack([lax.axis_index("ox"), lax.axis_index("oy")]).astype(jnp.int32)
    fields = (column_height, east_flow, north_flow, wet_mask)

    far_away = pl.BlockSpec(memory_space=pltpu.HBM)
    msg_a, msg_b, far_a, far_b, own = run(
        slip_kernel,
        [f32(ROW_MSG, LANES)] * 2 + [f32(16, LANES)] * 2 + [f32(3, RING, LANES)],
        [smem()] + [far_away] * 7,
        [
            pltpu.VMEM((9, 32, UX * LANES), jnp.bfloat16),
            pltpu.SMEM((1, 9), jnp.int32),
            pltpu.VMEM((STEPS, 32), jnp.bfloat16),
            pltpu.VMEM((3, 2, 8, COLS), jnp.float32),
            pltpu.VMEM((2, 8, COLS), jnp.int32),
            pltpu.SemaphoreType.DMA((19,)),
        ],
        (place,)
        + tuple(
            pltpu.with_memory_space_constraint(x, pltpu.HBM)
            for x in (intersection, slip_rate, jnp.transpose(green_kernel, (1, 0, 2))) + fields
        ),
        "slip",
    )
    got_a = swap(msg_a, "ox", 0)
    got_b = swap(msg_b, "ox", 1)
    gotfar_a = swap(far_a, "ox", 0, 2)
    gotfar_b = swap(far_b, "ox", 1, 2)

    side = [pl.BlockSpec((ROWS, LANES), lambda g: (0, 0)), pl.BlockSpec((ROWS, LANES), lambda g: (0, COLS // LANES - 1))]
    msg_a, msg_b, far_a, far_b, centre, ring, edges = run(
        column_kernel,
        [f32(COL_MSG, LANES)] * 2 + [f32(8, LANES)] * 2 + [f32(RING, LANES), f32(8, LANES), f32(4, 8, COLS)],
        [smem(), whole((3, RING, LANES))] + [whole((ROW_MSG, LANES))] * 2 + [whole((16, LANES))] * 2 + side * 4,
        [pltpu.VMEM((384, LANES), jnp.float32)],
        (place, own, got_a, got_b, gotfar_a, gotfar_b) + tuple(x for x in fields for _ in range(2)),
        "column",
    )
    got_a = swap(msg_a, "oy", 0)
    got_b = swap(msg_b, "oy", 1)
    gotfar_a = swap(far_a, "oy", 0, 2)
    gotfar_b = swap(far_b, "oy", 1, 2)

    tile = whole((ROWS, COLS))
    return tuple(
        run(
            step_kernel,
            [f32(ROWS, COLS)] * 3,
            [smem(), whole((RING, LANES))] + [whole((COL_MSG, LANES))] * 2 + [whole((8, LANES))] * 3
            + [whole((4, 8, COLS))] + [tile] * 4,
            [
                pltpu.VMEM((3, EXT, WIDE), jnp.float32),
                pltpu.VMEM((3, EXT, WIDE), jnp.float32),
                pltpu.VMEM((EXT, WIDE), jnp.float32),
                pltpu.VMEM((EXT, WIDE), jnp.float32),
                pltpu.VMEM((LANES, LANES), jnp.float32),
            ],
            (place, centre, got_a, got_b, gotfar_a, gotfar_b, ring, edges) + fields[:3] + (wet_mask,),
            "step",
        )
    )


def solution(mesh):
    return jax.shard_map(
        shards,
        mesh=mesh,
        in_specs=(
            P(None, ("ox", "oy")),
            P(("ox", "oy"), None, None),
            P(("ox", "oy"), None),
            P("ox", "oy"),
            P("ox", "oy"),
            P("ox", "oy"),
            P("ox", "oy"),
        ),
        out_specs=(P("ox", "oy"), P("ox", "oy"), P("ox", "oy")),
        check_vma=False,
    )
```

profile of v0, /device:TPU:4, one launch (start us, length us, event | category | flops | bytes accessed | tf_op | source)
XLA Modules:
  0.0 49.1 jit_solution(13975581201212464885)
XLA Ops:
  0.6 0.0 copy-start.2
  0.6 0.0 copy-start.1
  0.7 0.0 copy-start
  0.7 0.0 copy-start.3
  0.7 0.1 pad_add_fusion.place
  0.8 3.4 %slip.1 = (f32[848,128]{1,0:T(8,128)S(1)}, f32[848,128]{1,0:T(8,128)S(1)}, f32[16,128]{1,0:T(8,128)S(1)}, f32[16,128]{1,0:T(8,128)S(1)}, f32[3,264,128]{2,1,0:T(8,128)S(1)}) custom-call(s32[2]{0:T(128)S(1)} %pad_add_fusion.place, s32[1,9]{1,0:T(1,128)} %cover_in.1, bf16[4,32]{1,0:T(4,128)(2,1)} %slip_in.1, bf16[9,32,8192]{2,1,0:T(8,128)(2,1)} %bitcast.3, ...), custom_call_target="tpu_custom_call" | custom-call | tf_op jit(solution)/shard_map/slip/pallas_call | solution.py:402
  4.2 0.1 collective-permute-start
  4.3 4.5 %collective-permute-start.1 = (f32[848,128]{1,0:T(8,128)S(1)}, f32[848,128]{1,0:T(8,128)S(1)}, u32[]{:S(2)}, u32[]{:S(2)}) collective-permute-start(f32[848,128]{1,0:T(8,128)S(1)} %get-tuple-element.17), channel_id=1, source_target_pairs={{0,240},{16,32},{32,16},{48,64},{64,48},{80,96},{96,80},{112,128},... | collective-permute-start | bytes 1302536 | tf_op jit(solution)/shard_map/ppermute | solution.py:37
  8.7 0.0 collective-permute-start.2
  8.7 2.2 %collective-permute-start.3 = (f32[16,128]{1,0:T(8,128)S(1)}, f32[16,128]{1,0:T(8,128)S(1)}, u32[]{:S(2)}, u32[]{:S(2)}) collective-permute-start(f32[16,128]{1,0:T(8,128)S(1)} %get-tuple-element.19), channel_id=1, source_target_pairs={{0,224},{16,240},{32,64},{48,80},{64,32},{80,48},{96,128},{112,144... | collective-permute-start | bytes 24584 | tf_op jit(solution)/shard_map/ppermute | solution.py:37
  10.9 6.1 %collective-permute-done.2.gotfar_a = f32[16,128]{1,0:T(8,128)S(1)} collective-permute-done((f32[16,128]{1,0:T(8,128)S(1)}, f32[16,128]{1,0:T(8,128)S(1)}, u32[]{:S(2)}, u32[]{:S(2)}) %collective-permute-start.2) | collective-permute-done | bytes 8224 | tf_op jit(solution)/shard_map/ppermute | solution.py:37
  17.1 2.6 %collective-permute-done.3.gotfar_b = f32[16,128]{1,0:T(8,128)S(1)} collective-permute-done((f32[16,128]{1,0:T(8,128)S(1)}, f32[16,128]{1,0:T(8,128)S(1)}, u32[]{:S(2)}, u32[]{:S(2)}) %collective-permute-start.3) | collective-permute-done | bytes 8224 | tf_op jit(solution)/shard_map/ppermute | solution.py:37
  19.6 0.0 collective-permute-done.got_a
  19.6 0.0 collective-permute-done.1.got_b
  19.7 1.2 %column.1 = (f32[312,128]{1,0:T(8,128)S(1)}, f32[312,128]{1,0:T(8,128)S(1)}, f32[8,128]{1,0:T(8,128)S(1)}, f32[8,128]{1,0:T(8,128)S(1)}, f32[264,128]{1,0:T(8,12...) custom-call(s32[2]{0:T(128)S(1)} %pad_add_fusion.place, f32[3,264,128]{2,1,0:T(8,128)S(1)} %get-tuple-element.15.own, ...), custom_call_target="tpu_custom_call" | custom-call | tf_op jit(solution)/shard_map/column/pallas_call | solution.py:402
  20.9 1.3 %collective-permute-start.4 = (f32[312,128]{1,0:T(8,128)S(1)}, f32[312,128]{1,0:T(8,128)S(1)}, u32[]{:S(2)}, u32[]{:S(2)}) collective-permute-start(f32[312,128]{1,0:T(8,128)S(1)} %get-tuple-element.21), channel_id=1, source_target_pairs={{0,1},{1,0},{2,3},{3,2},{4,5},{5,4},{6,7},{7,6},{8,9},{9,8},{10,11... | collective-permute-start | bytes 479240 | tf_op jit(solution)/shard_map/ppermute | solution.py:37
  22.1 0.1 collective-permute-start.5
  22.2 8.0 %collective-permute-start.6 = (f32[8,128]{1,0:T(8,128)S(1)}, f32[8,128]{1,0:T(8,128)S(1)}, u32[]{:S(2)}, u32[]{:S(2)}) collective-permute-start(f32[8,128]{1,0:T(8,128)S(1)} %get-tuple-element.23), channel_id=1, source_target_pairs={{0,2},{1,3},{2,0},{3,1},{4,6},{5,7},{6,4},{7,5},{8,10},{9,11},{10,... | collective-permute-start | bytes 12296 | tf_op jit(solution)/shard_map/ppermute | solution.py:37
  30.2 0.0 collective-permute-start.7
  30.3 1.6 %collective-permute-done.6.gotfar_a = f32[8,128]{1,0:T(8,128)S(1)} collective-permute-done((f32[8,128]{1,0:T(8,128)S(1)}, f32[8,128]{1,0:T(8,128)S(1)}, u32[]{:S(2)}, u32[]{:S(2)}) %collective-permute-start.6) | collective-permute-done | bytes 4128 | tf_op jit(solution)/shard_map/ppermute | solution.py:37
  31.8 5.3 %collective-permute-done.7.gotfar_b = f32[8,128]{1,0:T(8,128)S(1)} collective-permute-done((f32[8,128]{1,0:T(8,128)S(1)}, f32[8,128]{1,0:T(8,128)S(1)}, u32[]{:S(2)}, u32[]{:S(2)}) %collective-permute-start.7) | collective-permute-done | bytes 4128 | tf_op jit(solution)/shard_map/ppermute | solution.py:37
  37.2 0.0 collective-permute-done.4.got_a
  37.2 0.0 collective-permute-done.5.got_b
  37.2 11.9 %step.1 = (f32[256,512]{1,0:T(8,128)}, f32[256,512]{1,0:T(8,128)}, f32[256,512]{1,0:T(8,128)}) custom-call(s32[2]{0:T(128)S(1)} %pad_add_fusion.place, f32[264,128]{1,0:T(8,128)S(1)} %get-tuple-element.20.centre, f32[312,128]{1,0:T(8,128)S(1)} %collective-permute-done.4.got_a, f32[312,128]{1,0:T(8,128)S(1)} %collective-permute-done.5.got_b, ...), custom_call_target="tpu_custom_call" | custom-call | tf_op jit(solution)/shard_map/step/pallas_call | solution.py:402
  (4 shorter events, 0.0 us)
Async XLA Ops:
  0.6 19.0 %copy-start.2 = (f32[256,512]{1,0:T(8,128)S(1)}, f32[256,512]{1,0:T(8,128)}, u32[]{:S(2)}) copy-start(f32[256,512]{1,0:T(8,128)} %n_in.3) | copy-start | bytes 1572868
  0.6 19.0 %copy-start.1 = (f32[256,512]{1,0:T(8,128)S(1)}, f32[256,512]{1,0:T(8,128)}, u32[]{:S(2)}) copy-start(f32[256,512]{1,0:T(8,128)} %m_in.3) | copy-start | bytes 1572868
  0.7 19.0 %copy-start = (f32[256,512]{1,0:T(8,128)S(1)}, f32[256,512]{1,0:T(8,128)}, u32[]{:S(2)}) copy-start(f32[256,512]{1,0:T(8,128)} %h_in.3) | copy-start | bytes 1572868
  0.7 19.0 %copy-start.3 = (s32[256,512]{1,0:T(8,128)S(1)}, s32[256,512]{1,0:T(8,128)}, u32[]{:S(2)}) copy-start(s32[256,512]{1,0:T(8,128)} %w_in.3) | copy-start | bytes 1572868
  4.2 15.5 %collective-permute-start = (f32[848,128]{1,0:T(8,128)S(1)}, f32[848,128]{1,0:T(8,128)S(1)}, u32[]{:S(2)}, u32[]{:S(2)}) collective-permute-start(f32[848,128]{1,0:T(8,128)S(1)} %get-tuple-element.16), channel_id=1, source_target_pairs={{0,16},{16,0},{32,48},{48,32},{64,80},{80,64},{96,112},{112,96},{1... | collective-permute-start | bytes 1302536 | tf_op jit(solution)/shard_map/ppermute | solution.py:37
  4.3 15.4 %collective-permute-start.1 = (f32[848,128]{1,0:T(8,128)S(1)}, f32[848,128]{1,0:T(8,128)S(1)}, u32[]{:S(2)}, u32[]{:S(2)}) collective-permute-start(f32[848,128]{1,0:T(8,128)S(1)} %get-tuple-element.17), channel_id=1, source_target_pairs={{0,240},{16,32},{32,16},{48,64},{64,48},{80,96},{96,80},{112,128},... | collective-permute-start | bytes 1302536 | tf_op jit(solution)/shard_map/ppermute | solution.py:37
  8.7 8.3 %collective-permute-start.2 = (f32[16,128]{1,0:T(8,128)S(1)}, f32[16,128]{1,0:T(8,128)S(1)}, u32[]{:S(2)}, u32[]{:S(2)}) collective-permute-start(f32[16,128]{1,0:T(8,128)S(1)} %get-tuple-element.18), channel_id=1, source_target_pairs={{0,32},{16,48},{32,0},{48,16},{64,96},{80,112},{96,64},{112,80},{1... | collective-permute-start | bytes 24584 | tf_op jit(solution)/shard_map/ppermute | solution.py:37
  8.7 10.9 %collective-permute-start.3 = (f32[16,128]{1,0:T(8,128)S(1)}, f32[16,128]{1,0:T(8,128)S(1)}, u32[]{:S(2)}, u32[]{:S(2)}) collective-permute-start(f32[16,128]{1,0:T(8,128)S(1)} %get-tuple-element.19), channel_id=1, source_target_pairs={{0,224},{16,240},{32,64},{48,80},{64,32},{80,48},{96,128},{112,144... | collective-permute-start | bytes 24584 | tf_op jit(solution)/shard_map/ppermute | solution.py:37
  20.9 16.3 %collective-permute-start.4 = (f32[312,128]{1,0:T(8,128)S(1)}, f32[312,128]{1,0:T(8,128)S(1)}, u32[]{:S(2)}, u32[]{:S(2)}) collective-permute-start(f32[312,128]{1,0:T(8,128)S(1)} %get-tuple-element.21), channel_id=1, source_target_pairs={{0,1},{1,0},{2,3},{3,2},{4,5},{5,4},{6,7},{7,6},{8,9},{9,8},{10,11... | collective-permute-start | bytes 479240 | tf_op jit(solution)/shard_map/ppermute | solution.py:37
  22.1 15.0 %collective-permute-start.5 = (f32[312,128]{1,0:T(8,128)S(1)}, f32[312,128]{1,0:T(8,128)S(1)}, u32[]{:S(2)}, u32[]{:S(2)}) collective-permute-start(f32[312,128]{1,0:T(8,128)S(1)} %get-tuple-element.22), channel_id=1, source_target_pairs={{0,15},{1,2},{2,1},{3,4},{4,3},{5,6},{6,5},{7,8},{8,7},{9,10},{10,... | collective-permute-start | bytes 479240 | tf_op jit(solution)/shard_map/ppermute | solution.py:37
  22.2 9.6 %collective-permute-start.6 = (f32[8,128]{1,0:T(8,128)S(1)}, f32[8,128]{1,0:T(8,128)S(1)}, u32[]{:S(2)}, u32[]{:S(2)}) collective-permute-start(f32[8,128]{1,0:T(8,128)S(1)} %get-tuple-element.23), channel_id=1, source_target_pairs={{0,2},{1,3},{2,0},{3,1},{4,6},{5,7},{6,4},{7,5},{8,10},{9,11},{10,... | collective-permute-start | bytes 12296 | tf_op jit(solution)/shard_map/ppermute | solution.py:37
  30.2 6.9 %collective-permute-start.7 = (f32[8,128]{1,0:T(8,128)S(1)}, f32[8,128]{1,0:T(8,128)S(1)}, u32[]{:S(2)}, u32[]{:S(2)}) collective-permute-start(f32[8,128]{1,0:T(8,128)S(1)} %get-tuple-element.24), channel_id=1, source_target_pairs={{0,14},{1,15},{2,4},{3,5},{4,2},{5,3},{6,8},{7,9},{8,6},{9,7},{10,... | collective-permute-start | bytes 12296 | tf_op jit(solution)/shard_map/ppermute | solution.py:37
where the time goes:
time: 49.1 us
  Pallas kernels  16.5 us (34%)
  starting transfers between devices  16.1 us (33%)
  waiting for transfers between devices  15.6 us (32%)
  between operations  0.72 us (1%)
    pallas_call x3, Pallas kernels, run(): pl.pallas_call(body, grid=(1,), in_specs=in_specs, out_specs=[whole(o.sha...  16.5 us
    ppermute x8, starting transfers between devices, swap(): return lax.ppermute(value, axis, partners(axis, parity, reach))  16.1 us
    ppermute x8, waiting for transfers between devices, swap(): return lax.ppermute(value, axis, partners(axis, parity, reach))  15.6 us
  transfers between devices with their start and end apart: 8, of which 4 were waited for; matrix products, arithmetic and copies ran while one was open for 0% of the time, Pallas kernels for 0%

commit v1 on v0

v1 whole, which is shorter than its diff:
```python
import functools

import jax
import jax.numpy as jnp
from jax import lax
from jax.experimental import pallas as pl
from jax.experimental.pallas import tpu as pltpu
from jax.sharding import PartitionSpec as P

STEPS = 4
SIDE = 16
ROWS = 256
COLS = 512
LANES = 128
UX = 64
MAIN = STEPS * UX
RING = MAIN + 8
SLIVER = 2 * MAIN
EDGE = SLIVER + 16
RIM = EDGE + 64
ROW_MSG = RIM + 8
TURNED = RING
COL_MSG = RING + 48
MID_MSG = COL_MSG + 8
TALL = 3 * LANES
UNROLL = 4
VMEM_LIMIT = 48 * 1024 * 1024


def partners(axis, parity, reach):
    return [
        (i, (i + reach if (i // reach) % 2 == parity else i - reach) % SIDE)
        for i in range(SIDE)
    ]


def swap(value, axis, parity, reach=1):
    return lax.ppermute(value, axis, partners(axis, parity, reach))


def slip_kernel(
    place, cover_in, slip_in, green, h_in, m_in, n_in, w_in,
    msg_a, msg_b, mid_a, mid_b, far_a, far_b, own, rim, held, cover, slip, edge_f, edge_i, lanes, sems,
):
    def fetch(slot):
        return pltpu.make_async_copy(green.at[slot], held.at[slot], sems.at[slot])

    small = [
        pltpu.make_async_copy(slip_in, slip, sems.at[9]),
        pltpu.make_async_copy(cover_in, cover, sems.at[10]),
    ]
    edges = []
    for f, field in enumerate((h_in, m_in, n_in, w_in)):
        for t, start in enumerate((0, ROWS - 8)):
            target = edge_f.at[f, t] if f < 3 else edge_i.at[t]
            edges.append(
                pltpu.make_async_copy(field.at[start : start + 8], target, sems.at[11 + 2 * f + t])
            )
    for copy in small:
        copy.start()
    order = (0, 6, 3, 1, 7, 4, 2, 8, 5)
    for slot in order:
        fetch(slot).start()
    for copy in edges:
        copy.start()
    for copy in small:
        copy.wait()
    even = place[0] % 2 == 0
    even2 = (place[0] // 2) % 2 == 0

    rates = slip[...].astype(jnp.float32)
    rates = jnp.concatenate([rates] * 8, axis=1)
    rates = jnp.concatenate(
        [jnp.broadcast_to(rates[s : s + 1], (8, 256)) for s in range(STEPS)], axis=0
    )
    row = lax.broadcasted_iota(jnp.int32, (32, 256), 0)
    col = lax.broadcasted_iota(jnp.int32, (32, 256), 1)
    spread = jnp.where(col // 32 == row % 8, rates, 0.0).astype(jnp.bfloat16)
    lane = lax.broadcasted_iota(jnp.int32, (32, LANES), 1)

    def group(slot, g):
        right = jnp.concatenate(
            [held[slot, :, (g * 8 + p) * LANES : (g * 8 + p + 1) * LANES] for p in range(8)],
            axis=0,
        )
        value = jnp.dot(spread, right, preferred_element_type=jnp.float32)
        return value * cover[0, slot].astype(jnp.float32)

    def rims(down, up, mid):
        value = jnp.where(lane == 1, pltpu.roll(up, 1, 1), down)
        value = jnp.where(lane == LANES - 2, pltpu.roll(up, LANES - 1, 1), value)
        value = jnp.where(lane == 2, pltpu.roll(mid, 2, 1), value)
        return jnp.where(lane == LANES - 3, pltpu.roll(mid, LANES - 2, 1), value)

    for b in range(3):
        fetch(b).wait()
        fetch(6 + b).wait()
        fetch(3 + b).wait()
        to_a, to_b, base = ((msg_a, msg_b, 0), (mid_a, mid_b, 0), (msg_a, msg_b, MAIN))[b]
        for g in range(8):
            up = group(b, g)
            down = group(6 + b, g)
            mid = group(3 + b, g)
            first = jnp.where(even, down, up)
            second = jnp.where(even, up, down)
            if b == 1:
                rim_lanes = rims(down, up, mid)
            for s in range(STEPS):
                part = slice(8 * s, 8 * s + 8)
                at = s * UX + g * 8
                to_a[base + at : base + at + 8, :] = first[part]
                to_b[base + at : base + at + 8, :] = second[part]
                own[b, at : at + 8, :] = mid[part]
                if b == 1:
                    lanes[at : at + 8, :] = rim_lanes[part]
            if g == 0:
                for s in range(STEPS):
                    own[b, MAIN + s : MAIN + s + 1, :] = down[8 * s : 8 * s + 1]
                up_edge, up_mid = up, mid
            if g == 7:
                for s in range(STEPS):
                    own[b, MAIN + 4 + s : MAIN + 5 + s, :] = up[8 * s + 7 : 8 * s + 8]
                    at = b * STEPS + s
                    to_down = mid[8 * s + 7 : 8 * s + 8]
                    to_up = up_mid[8 * s : 8 * s + 1]
                    msg_a[SLIVER + at : SLIVER + at + 1, :] = jnp.where(even, to_down, to_up)
                    msg_b[SLIVER + at : SLIVER + at + 1, :] = jnp.where(even, to_up, to_down)
                    to_down = down[8 * s + 7 : 8 * s + 8]
                    to_up = up_edge[8 * s : 8 * s + 1]
                    far_a[at : at + 1, :] = jnp.where(even2, to_down, to_up)
                    far_b[at : at + 1, :] = jnp.where(even2, to_up, to_down)
    blank = jnp.zeros((4, LANES), jnp.float32)
    for ref, start in ((msg_a, SLIVER + 12), (msg_b, SLIVER + 12), (far_a, 12), (far_b, 12)):
        ref[start : start + 4, :] = blank
    for ref, start in ((msg_a, RIM + 4), (msg_b, RIM + 4), (rim, 4)):
        ref[start : start + 4, :] = blank
    for ref in (mid_a, mid_b):
        ref[MAIN:MID_MSG, :] = jnp.zeros((MID_MSG - MAIN, LANES), jnp.float32)
    for k in range(2):
        turned = lanes[k * LANES : (k + 1) * LANES, :].T
        to_down = jnp.concatenate([turned[0:1], turned[127:128]], axis=0)
        to_up = jnp.concatenate([turned[1:2], turned[126:127]], axis=0)
        at = RIM + 2 * k
        msg_a[at : at + 2, :] = jnp.where(even, to_down, to_up)
        msg_b[at : at + 2, :] = jnp.where(even, to_up, to_down)
        rim[2 * k : 2 * k + 1, :] = turned[2:3]
        rim[2 * k + 1 : 2 * k + 2, :] = turned[125:126]

    for copy in edges:
        copy.wait()
    for f in range(4):
        top, bottom = (edge_f[f, 0], edge_f[f, 1]) if f < 3 else (edge_i[0], edge_i[1])
        to_up = top[0:4].astype(jnp.float32)
        to_down = bottom[4:8].astype(jnp.float32)
        first = jnp.where(even, to_down, to_up)
        second = jnp.where(even, to_up, to_down)
        for k in range(4):
            at = EDGE + (f * 4 + k) * 4
            msg_a[at : at + 4, :] = first[:, k * LANES : (k + 1) * LANES]
            msg_b[at : at + 4, :] = second[:, k * LANES : (k + 1) * LANES]


def column_kernel(
    place, _, own, rim, got_a, got_b, gotfar_a, gotfar_b, h_l, h_r, m_l, m_r, n_l, n_r, w_l, w_r,
    msg_a, msg_b, far_a, far_b, tail1, ring, turned_own, edges, lanes,
):
    i, j = place[0], place[1]
    even = i % 2 == 0
    even2 = (i // 2) % 2 == 0
    above_ok, below_ok = i > 0, i < SIDE - 1
    above2_ok, below2_ok = i > 1, i < SIDE - 2
    even_j = j % 2 == 0
    even2_j = (j // 2) % 2 == 0

    def from_above(rows):
        return jnp.where(even, got_b[rows, :], got_a[rows, :])

    def from_below(rows):
        return jnp.where(even, got_a[rows, :], got_b[rows, :])

    tails = []
    for b in range(3):
        rows = slice(SLIVER + 4 * b, SLIVER + 4 * b + 4)
        far = slice(4 * b, 4 * b + 4)
        above = jnp.where(above_ok, from_above(rows), 0.0)
        above = above + jnp.where(
            above2_ok, jnp.where(even2, gotfar_b[far, :], gotfar_a[far, :]), 0.0
        )
        below = jnp.where(below_ok, from_below(rows), 0.0)
        below = below + jnp.where(
            below2_ok, jnp.where(even2, gotfar_a[far, :], gotfar_b[far, :]), 0.0
        )
        tails.append(own[b, MAIN:RING, :] + jnp.concatenate([below, above], axis=0))
    tail1[...] = tails[1]

    sums = []
    for b, base in ((0, 0), (2, MAIN)):
        rows = slice(base, base + MAIN)
        main = own[b, 0:MAIN, :]
        main = main + jnp.where(above_ok, from_above(rows), 0.0)
        main = main + jnp.where(below_ok, from_below(rows), 0.0)
        sums.append(main)
    left_sum, right_sum = sums
    msg_a[0:MAIN, :] = jnp.where(even_j, right_sum, left_sum)
    msg_b[0:MAIN, :] = jnp.where(even_j, left_sum, right_sum)
    msg_a[MAIN:RING, :] = jnp.where(even_j, tails[2], tails[0])
    msg_b[MAIN:RING, :] = jnp.where(even_j, tails[0], tails[2])

    for f in range(4):
        for k in range(4):
            rows = slice(EDGE + (f * 4 + k) * 4, EDGE + (f * 4 + k) * 4 + 4)
            edges[f, :, k * LANES : (k + 1) * LANES] = jnp.concatenate(
                [from_below(rows), from_above(rows)], axis=0
            )

    def tuck(packed, lane, block, source, target, count):
        moved = pltpu.roll(block, (target - source) % LANES, 1) if target != source else block
        return jnp.where((lane >= target) & (lane < target + count), moved, packed)

    fields = ((h_l, h_r), (m_l, m_r), (n_l, n_r), (w_l, w_r))
    lane = lax.broadcasted_iota(jnp.int32, (ROWS, LANES), 1)
    packed = jnp.zeros((ROWS, LANES), jnp.float32)
    lane8 = lax.broadcasted_iota(jnp.int32, (8, LANES), 1)
    packed8 = jnp.zeros((8, LANES), jnp.float32)
    for f, (left, right) in enumerate(fields):
        packed = tuck(packed, lane, right[...].astype(jnp.float32), LANES - 8, 8 * f, 8)
        packed = tuck(packed, lane, left[...].astype(jnp.float32), 0, 32 + 8 * f, 8)
        packed8 = tuck(packed8, lane8, edges[f, :, COLS - LANES : COLS], LANES - 8, 8 * f, 8)
        packed8 = tuck(packed8, lane8, edges[f, :, 0:LANES], 0, 32 + 8 * f, 8)
    spots = ((2, LANES - 1, 64), (0, 0, 65), (0, LANES - 1, 66), (2, 0, 67))
    for b, source, target in spots:
        packed = tuck(packed, lane, sums[b // 2], source, target, 1)
        packed8 = tuck(packed8, lane8, tails[b], source, target, 1)
    packed8 = tuck(packed8, lane8, tails[1], 0, 68, 1)
    packed8 = tuck(packed8, lane8, tails[1], LANES - 1, 69, 1)
    lanes[0:ROWS, :] = packed
    lanes[ROWS : ROWS + 4, :] = packed8[0:4]
    lanes[ROWS + 4 : TALL - 4, :] = jnp.zeros((TALL - ROWS - 8, LANES), jnp.float32)
    lanes[TALL - 4 : TALL, :] = packed8[4:8]

    zero8 = jnp.zeros((8, LANES), jnp.float32)
    far_a[...] = zero8
    far_b[...] = zero8
    ring[...] = zero8
    for k in range(3):
        turned = lanes[k * LANES : (k + 1) * LANES, :].T
        turned_own[k] = turned[0:64]
        if k < 2:
            rims = []
            for side in range(2):
                row = slice(RIM + 2 * k + side, RIM + 2 * k + side + 1)
                value = rim[2 * k + side : 2 * k + side + 1, :]
                value = value + jnp.where(above_ok, from_above(row), 0.0)
                rims.append(value + jnp.where(below_ok, from_below(row), 0.0))
        else:
            rims = [turned[68:69], turned[69:70]]
        to_right = [turned[8 * f + 4 : 8 * f + 8] for f in range(3)] + [rims[1], turned[29:32]]
        to_left = [turned[32 + 8 * f : 36 + 8 * f] for f in range(3)] + [turned[56:59], rims[0]]
        to_right = jnp.concatenate(to_right, axis=0)
        to_left = jnp.concatenate(to_left, axis=0)
        at = TURNED + 16 * k
        msg_a[at : at + 16, :] = jnp.where(even_j, to_right, to_left)
        msg_b[at : at + 16, :] = jnp.where(even_j, to_left, to_right)
        far_a[k : k + 1, :] = jnp.where(even2_j, turned[64:65], turned[65:66])
        far_b[k : k + 1, :] = jnp.where(even2_j, turned[65:66], turned[64:65])
        ring[k : k + 1, :] = turned[66:67]
        ring[4 + k : 5 + k, :] = turned[67:68]


def spread_matrix():
    coarse = lax.broadcasted_iota(jnp.int32, (LANES, COLS), 0)
    fine = lax.broadcasted_iota(jnp.int32, (LANES, COLS), 1)
    return jnp.where(fine // 4 == coarse, 1.0, 0.0).astype(jnp.bfloat16)


def widen(value, spread):
    part = value.astype(jnp.bfloat16)
    rest = value - part.astype(jnp.float32)
    part2 = rest.astype(jnp.bfloat16)
    part3 = (rest - part2.astype(jnp.float32)).astype(jnp.bfloat16)
    dot = functools.partial(jnp.dot, preferred_element_type=jnp.float32)
    return dot(part, spread) + dot(part2, spread) + dot(part3, spread)


def fluxes(height, east, north):
    inverse = 1.0 / height
    v = north * inverse
    pressure = 0.05 * height * height
    fm = 0.1 * east
    gn = 0.1 * north
    fmm = fm * (east * inverse) + pressure
    fmn = fm * v
    gnn = gn * v + pressure
    quarter = (0.25 * height, 0.25 * east, 0.25 * north)
    return quarter, (fm, fmm, fmn), (gn, fmn, gnn)


def interior_step(load, store):
    sub = lax.broadcasted_iota(jnp.int32, (8, COLS), 0)
    first_row, last_row = sub == 0, sub == 7
    zeros = jnp.zeros((8, COLS), jnp.float32)

    def finish(at, partial, ahead):
        store(at, [p + jnp.where(last_row, u, 0.0) for p, u in zip(partial, ahead)])

    def body(c, carry):
        partial, above = carry
        at = pl.multiple_of(c * 8, 8)
        quarter, east_flux, north_flux = fluxes(*load(at))
        below = [pltpu.roll(q + x, 1, 0) for q, x in zip(quarter, east_flux)]
        ahead = [pltpu.roll(q - x, 7, 0) for q, x in zip(quarter, east_flux)]
        new_partial = [
            pltpu.roll(q - g, COLS - 1, 1)
            + pltpu.roll(q + g, 1, 1)
            + jnp.where(first_row, a, b)
            + jnp.where(last_row, 0.0, u)
            for q, g, a, b, u in zip(quarter, north_flux, above, below, ahead)
        ]
        finish(pl.multiple_of(jnp.maximum(c - 1, 0) * 8, 8), partial, ahead)
        return new_partial, below

    partial, _ = lax.fori_loop(0, ROWS // 8, body, ([zeros] * 3, [zeros] * 3), unroll=UNROLL)
    finish(ROWS - 8, partial, [zeros] * 3)


def first_kernel(h_in, m_in, n_in, moved):
    def load(at):
        return [ref[pl.ds(at, 8), :] for ref in (h_in, m_in, n_in)]

    def store(at, values):
        for f in range(3):
            moved[f, pl.ds(at, 8), :] = values[f]

    interior_step(load, store)


def main_kernel(
    place, own, mid_a, mid_b, got_a, got_b, moved, w_in,
    h_out, m_out, n_out, total, state, lift,
):
    i, j = place[0], place[1]
    even = i % 2 == 0
    even_j = j % 2 == 0
    rows = slice(0, MAIN)
    value = own[1, rows, :]
    value = value + jnp.where(i > 0, jnp.where(even, mid_b[rows, :], mid_a[rows, :]), 0.0)
    value = value + jnp.where(i < SIDE - 1, jnp.where(even, mid_a[rows, :], mid_b[rows, :]), 0.0)
    value = value + jnp.where(j > 0, jnp.where(even_j, got_b[rows, :], got_a[rows, :]), 0.0)
    value = value + jnp.where(
        j < SIDE - 1, jnp.where(even_j, got_a[rows, :], got_b[rows, :]), 0.0
    )
    total[...] = 0.05 * value
    lift[...] = widen(total[...], spread_matrix())
    upper_half = lax.broadcasted_iota(jnp.int32, (8, COLS), 0) < 4

    def source_and_mask(s, at, values):
        row = s * UX + at // 4
        raised = jnp.where(
            upper_half,
            jnp.broadcast_to(lift[pl.ds(row, 1), :], (8, COLS)),
            jnp.broadcast_to(lift[pl.ds(row + 1, 1), :], (8, COLS)),
        )
        mask = w_in[pl.ds(at, 8), :].astype(jnp.float32)
        return [values[0] + raised, values[1] * mask, values[2] * mask]

    for s in range(1, STEPS):

        def load(at, s=s):
            if s == 1:
                return source_and_mask(0, at, [moved[f, pl.ds(at, 8), :] for f in range(3)])
            return [state[s % 2, f, pl.ds(at, 8), :] for f in range(3)]

        def store(at, values, s=s):
            values = source_and_mask(s, at, values)
            for f in range(3):
                if s == STEPS - 1:
                    (h_out, m_out, n_out)[f][pl.ds(at, 8), :] = values[f]
                else:
                    state[(s + 1) % 2, f, pl.ds(at, 8), :] = values[f]

        interior_step(load, store)


def strip_kernel(
    place, total, tail1, got_a, got_b, gotfar_a, gotfar_b, ring, turned_own, edges,
    h_t, h_b, m_t, m_b, n_t, n_b, w_t, w_b, h_in, m_in, n_in,
    h_out, m_out, n_out, block,
):
    i, j = place[0], place[1]
    even_j = j % 2 == 0
    even2_j = (j // 2) % 2 == 0
    spread = spread_matrix()

    def from_left(rows):
        return jnp.where(even_j, got_b[rows, :], got_a[rows, :])

    def from_right(rows):
        return jnp.where(even_j, got_a[rows, :], got_b[rows, :])

    tail = tail1[...] + jnp.where(j > 0, from_left(slice(MAIN, RING)), 0.0)
    tail = 0.05 * (tail + jnp.where(j < SIDE - 1, from_right(slice(MAIN, RING)), 0.0))

    def six(values):
        return jnp.concatenate([jnp.broadcast_to(v, (4, v.shape[1])) for v in values], axis=0)

    coarse = []
    for s in range(STEPS):
        at = s * UX
        coarse += [
            tail[4 + s : 5 + s], total[at : at + 2, :], total[at + UX - 2 : at + UX, :], tail[s : s + 1],
        ]
    fine = widen(jnp.concatenate(coarse, axis=0), spread)
    row_lift = [
        six([fine[6 * s + r : 6 * s + r + 1] for r in range(6)]) for s in range(STEPS)
    ]
    row_state = []
    for f, (top, bottom) in enumerate(((h_t, h_b), (m_t, m_b), (n_t, n_b), (w_t, w_b))):
        row_state.append(
            jnp.concatenate(
                [
                    edges[f, 4:8, :],
                    top[...].astype(jnp.float32),
                    bottom[...].astype(jnp.float32),
                    edges[f, 0:4, :],
                ],
                axis=0,
            )
        )

    parts = [[], [], [], []]
    ups = []
    for k in range(3):
        at = TURNED + 16 * k
        left, right = from_left(slice(at, at + 16)), from_right(slice(at, at + 16))
        for f in range(4):
            parts[f].append(
                jnp.concatenate(
                    [
                        left[4 * f : 4 * f + 4],
                        turned_own[k, 32 + 8 * f : 40 + 8 * f, :],
                        turned_own[k, 8 * f : 8 * f + 8, :],
                        right[4 * f : 4 * f + 4],
                    ],
                    axis=0,
                )
            )
        far_left = jnp.where(even2_j, gotfar_b[k : k + 1, :], gotfar_a[k : k + 1, :])
        far_right = jnp.where(even2_j, gotfar_a[k : k + 1, :], gotfar_b[k : k + 1, :])
        ring_left = ring[k : k + 1, :] + left[12:13] + jnp.where(j > 1, far_left, 0.0)
        ring_right = ring[4 + k : 5 + k, :] + right[15:16]
        ring_right = ring_right + jnp.where(j < SIDE - 2, far_right, 0.0)
        if k < 2:
            turned = total[k * LANES : (k + 1) * LANES, :].T
        else:
            block[...] = jnp.zeros((LANES, LANES), jnp.float32)
            block[0:4, :] = tail[0:4]
            block[LANES - 4 : LANES, :] = tail[4:8]
            turned = block[...].T
        ups.append(
            jnp.concatenate(
                [0.05 * ring_left, turned[0:2], turned[126:128], 0.05 * ring_right, turned[0:2]],
                axis=0,
            )
        )
    col_state = [jnp.concatenate(p, axis=1) for p in parts]
    lane = lax.broadcasted_iota(jnp.int32, (8, LANES), 1)
    col_lift = []
    for s in range(STEPS):
        if s % 2 == 0:
            wide = widen(ups[s // 2], spread)
        own_rows = wide[:, 256 * (s % 2) : 256 * (s % 2) + 256]
        beside = jnp.where(
            lane < 4,
            jnp.broadcast_to(ups[2][:, s : s + 1], (8, LANES)),
            jnp.broadcast_to(ups[2][:, LANES - 4 + s : LANES - 3 + s], (8, LANES)),
        )
        both = jnp.concatenate([own_rows, beside], axis=1)
        col_lift.append(six([both[r : r + 1] for r in range(6)]))

    def advance(state, lift, wet, x_axis, ends):
        n_sub, n_lane = state[0].shape
        sub = lax.broadcasted_iota(jnp.int32, (n_sub, n_lane), 0)
        lanes = lax.broadcasted_iota(jnp.int32, (n_sub, n_lane), 1)
        fixed = []
        for value in state:
            value = jnp.where((sub == 3) & ends[0], pltpu.roll(value, n_sub - 1, 0), value)
            value = jnp.where((sub == 20) & ends[1], pltpu.roll(value, 1, 0), value)
            if len(ends) == 4:
                value = jnp.where((lanes == n_lane - 1) & ends[2], pltpu.roll(value, n_lane - 1, 1), value)
                value = jnp.where((lanes == ROWS) & ends[3], pltpu.roll(value, 1, 1), value)
            fixed.append(value)
        quarter, east_flux, north_flux = fluxes(*fixed)
        along_sub, along_lane = (east_flux, north_flux) if x_axis == 0 else (north_flux, east_flux)
        out = [
            pltpu.roll(q - a, n_sub - 1, 0)
            + pltpu.roll(q + a, 1, 0)
            + pltpu.roll(q - l, n_lane - 1, 1)
            + pltpu.roll(q + l, 1, 1)
            for q, a, l in zip(quarter, along_sub, along_lane)
        ]
        return [out[0] + lift, out[1] * wet, out[2] * wet]

    row_ends = (i == 0, i == SIDE - 1)
    col_ends = (j == 0, j == SIDE - 1) + row_ends
    rows, cols = row_state[:3], col_state[:3]
    for s in range(STEPS):
        rows = advance(rows, row_lift[s], row_state[3], 0, row_ends)
        cols = advance(cols, col_lift[s], col_state[3], 1, col_ends)

    lane = lax.broadcasted_iota(jnp.int32, (ROWS, LANES), 1)
    for f, (source, target) in enumerate(((h_in, h_out), (m_in, m_out), (n_in, n_out))):
        block[8 * f : 8 * f + 4, :] = cols[f][16:20, 0:LANES]
        block[8 * f + 4 : 8 * f + 8, :] = cols[f][4:8, 0:LANES]
    upper = block[...].T
    for f in range(3):
        block[8 * f : 8 * f + 4, :] = cols[f][16:20, LANES : 2 * LANES]
        block[8 * f + 4 : 8 * f + 8, :] = cols[f][4:8, LANES : 2 * LANES]
    rim = jnp.concatenate([upper, block[...].T], axis=0)
    for f, (source, target) in enumerate(((h_in, h_out), (m_in, m_out), (n_in, n_out))):
        value = jnp.concatenate(
            [rows[f][4:8], source[4 : ROWS - 4, :], rows[f][16:20]], axis=0
        )
        side = pltpu.roll(rim, (LANES - 4 - 8 * f) % LANES, 1)
        target[:, 0:LANES] = jnp.where(lane < 4, side, value[:, 0:LANES])
        target[:, LANES : COLS - LANES] = value[:, LANES : COLS - LANES]
        target[:, COLS - LANES : COLS] = jnp.where(
            lane >= LANES - 4, side, value[:, COLS - LANES : COLS]
        )


def whole(shape):
    return pl.BlockSpec(shape, lambda g: (0,) * len(shape))


def smem():
    return pl.BlockSpec(memory_space=pltpu.SMEM)


def f32(*shape):
    return jax.ShapeDtypeStruct(shape, jnp.float32)


def run(body, outs, in_specs, scratch, args, name, cost=None):
    if cost is not None:
        cost = pl.CostEstimate(flops=cost, bytes_accessed=0, transcendentals=0)
    return pl.pallas_call(
        body,
        grid=(1,),
        in_specs=in_specs,
        out_specs=[whole(o.shape) for o in outs],
        out_shape=outs,
        scratch_shapes=scratch,
        compiler_params=pltpu.CompilerParams(vmem_limit_bytes=VMEM_LIMIT),
        cost_estimate=cost,
        name=name,
    )(*args)


def shards(slip_rate, green_kernel, intersection, wet_mask, column_height, east_flow, north_flow):
    place = jnp.stack([lax.axis_index("ox"), lax.axis_index("oy")]).astype(jnp.int32)
    fields = (column_height, east_flow, north_flow, wet_mask)
    twice = tuple(x for x in fields for _ in range(2))

    far_away = pl.BlockSpec(memory_space=pltpu.HBM)
    msg_a, msg_b, mid_a, mid_b, far_a, far_b, own, rim = run(
        slip_kernel,
        [f32(ROW_MSG, LANES)] * 2 + [f32(MID_MSG, LANES)] * 2 + [f32(16, LANES)] * 2
        + [f32(3, RING, LANES), f32(8, LANES)],
        [smem()] + [far_away] * 7,
        [
            pltpu.VMEM((9, 32, UX * LANES), jnp.bfloat16),
            pltpu.SMEM((1, 9), jnp.int32),
            pltpu.VMEM((STEPS, 32), jnp.bfloat16),
            pltpu.VMEM((3, 2, 8, COLS), jnp.float32),
            pltpu.VMEM((2, 8, COLS), jnp.int32),
            pltpu.VMEM((MAIN, LANES), jnp.float32),
            pltpu.SemaphoreType.DMA((19,)),
        ],
        (place,)
        + tuple(
            pltpu.with_memory_space_constraint(x, pltpu.HBM)
            for x in (intersection, slip_rate, jnp.transpose(green_kernel, (1, 0, 2))) + fields
        ),
        "slip",
    )
    got_a = swap(msg_a, "ox", 0)
    got_b = swap(msg_b, "ox", 1)
    gotfar_a = swap(far_a, "ox", 0, 2)
    gotfar_b = swap(far_b, "ox", 1, 2)
    mid_a = swap(mid_a, "ox", 0)
    mid_b = swap(mid_b, "ox", 1)

    side = [
        pl.BlockSpec((ROWS, LANES), lambda g: (0, 0)),
        pl.BlockSpec((ROWS, LANES), lambda g: (0, COLS // LANES - 1)),
    ]
    tile = whole((ROWS, COLS))
    (moved,) = run(
        first_kernel, [f32(3, ROWS, COLS)], [tile] * 3, [], fields[:3], "first", None
    )
    msg_a, msg_b, far_a, far_b, tail1, ring, turned_own, edges = run(
        column_kernel,
        [f32(COL_MSG, LANES)] * 2 + [f32(8, LANES)] * 4 + [f32(3, 64, LANES), f32(4, 8, COLS)],
        [smem(), pl.BlockSpec(memory_space=pl.ANY), whole((3, RING, LANES)), whole((8, LANES))]
        + [whole((ROW_MSG, LANES))] * 2
        + [whole((16, LANES))] * 2 + side * 4,
        [pltpu.VMEM((TALL, LANES), jnp.float32)],
        (place, moved, own, rim, got_a, got_b, gotfar_a, gotfar_b) + twice,
        "column",
        10000000000,
    )
    got_a = swap(msg_a, "oy", 0)
    got_b = swap(msg_b, "oy", 1)
    gotfar_a = swap(far_a, "oy", 0, 2)
    gotfar_b = swap(far_b, "oy", 1, 2)

    height, east, north, total = run(
        main_kernel,
        [f32(ROWS, COLS)] * 3 + [f32(MAIN, LANES)],
        [smem(), whole((3, RING, LANES))] + [whole((MID_MSG, LANES))] * 2
        + [whole((COL_MSG, LANES))] * 2 + [whole((3, ROWS, COLS)), tile],
        [
            pltpu.VMEM((2, 3, ROWS, COLS), jnp.float32),
            pltpu.VMEM((MAIN, COLS), jnp.float32),
        ],
        (place, own, mid_a, mid_b, got_a, got_b, moved, wet_mask),
        "main",
        10000000000,
    )
    ends = [
        pl.BlockSpec((8, COLS), lambda g: (0, 0)),
        pl.BlockSpec((8, COLS), lambda g: (ROWS // 8 - 1, 0)),
    ]
    return tuple(
        run(
            strip_kernel,
            [f32(ROWS, COLS)] * 3,
            [smem(), whole((MAIN, LANES)), whole((8, LANES))] + [whole((COL_MSG, LANES))] * 2
            + [whole((8, LANES))] * 3 + [whole((3, 64, LANES)), whole((4, 8, COLS))] + ends * 4
            + [tile] * 3,
            [pltpu.VMEM((LANES, LANES), jnp.float32)],
            (place, total, tail1, got_a, got_b, gotfar_a, gotfar_b, ring, turned_own, edges)
            + twice + (height, east, north),
            "strip",
        )
    )


def solution(mesh):
    return jax.shard_map(
        shards,
        mesh=mesh,
        in_specs=(
            P(None, ("ox", "oy")),
            P(("ox", "oy"), None, None),
            P(("ox", "oy"), None),
            P("ox", "oy"),
            P("ox", "oy"),
            P("ox", "oy"),
            P("ox", "oy"),
        ),
        out_specs=(P("ox", "oy"), P("ox", "oy"), P("ox", "oy")),
        check_vma=False,
    )
```

time: 49.1 us -> 44.5 us (0.906)
  the two profiles are of different devices: /device:TPU:4 before, /device:TPU:25 now
where the time goes in v1:
time: 44.5 us; the launch traced here: 44.4 us
  starting transfers between devices  18 us (40%)
  Pallas kernels  16 us (36%)
  waiting for transfers between devices  9.51 us (21%)
  between operations  0.72 us (2%)
    ppermute x10, starting transfers between devices, swap(): return lax.ppermute(value, axis, partners(axis, parity, reach))  18 us
    pallas_call x5, Pallas kernels, run(): pl.pallas_call(body, grid=(1,), in_specs=in_specs, out_specs=[whole(o.sha...  16 us
    ppermute x10, waiting for transfers between devices, swap(): return lax.ppermute(value, axis, partners(axis, parity, reach))  9.51 us
  transfers between devices with their start and end apart: 10, of which 2 were waited for; matrix products, arithmetic and copies ran while one was open for 0% of the time, Pallas kernels for 21%

profile of v1, /device:TPU:25, one launch (start us, length us, event | category | flops | bytes accessed | tf_op | source)
XLA Modules:
  0.0 44.4 jit_solution(8620977323330319565)
XLA Ops:
  0.6 0.0 copy-start.2
  0.6 0.0 copy-start.1
  0.7 0.0 copy-start
  0.7 0.1 pad_add_fusion.place
  0.7 3.4 %slip.1 = (f32[600,128]{1,0:T(8,128)S(1)}, f32[600,128]{1,0:T(8,128)S(1)}, f32[320,128]{1,0:T(8,128)S(1)}, f32[320,128]{1,0:T(8,128)S(1)}, f32[16,128]{1,0:T(8,1...) custom-call(s32[2]{0:T(128)S(1)} %pad_add_fusion.place, s32[1,9]{1,0:T(1,128)} %cover_in.1, ...), custom_call_target="tpu_custom_call" | custom-call | tf_op jit(solution)/shard_map/slip/pallas_call | solution.py:546
  4.2 0.8 %collective-permute-start.2 = (f32[600,128]{1,0:T(8,128)S(1)}, f32[600,128]{1,0:T(8,128)S(1)}, u32[]{:S(2)}, u32[]{:S(2)}) collective-permute-start(f32[600,128]{1,0:T(8,128)S(1)} %get-tuple-element.27), channel_id=1, source_target_pairs={{0,16},{16,0},{32,48},{48,32},{64,80},{80,64},{96,112},{112,96},{1... | collective-permute-start | bytes 921608 | tf_op jit(solution)/shard_map/ppermute | solution.py:38
  4.9 1.6 %collective-permute-start.3 = (f32[600,128]{1,0:T(8,128)S(1)}, f32[600,128]{1,0:T(8,128)S(1)}, u32[]{:S(2)}, u32[]{:S(2)}) collective-permute-start(f32[600,128]{1,0:T(8,128)S(1)} %get-tuple-element.28), channel_id=1, source_target_pairs={{0,240},{16,32},{32,16},{48,64},{64,48},{80,96},{96,80},{112,128},... | collective-permute-start | bytes 921608 | tf_op jit(solution)/shard_map/ppermute | solution.py:38
  6.5 1.2 %collective-permute-start.4 = (f32[16,128]{1,0:T(8,128)S(1)}, f32[16,128]{1,0:T(8,128)S(1)}, u32[]{:S(2)}, u32[]{:S(2)}) collective-permute-start(f32[16,128]{1,0:T(8,128)S(1)} %get-tuple-element.29), channel_id=1, source_target_pairs={{0,32},{16,48},{32,0},{48,16},{64,96},{80,112},{96,64},{112,80},{1... | collective-permute-start | bytes 24584 | tf_op jit(solution)/shard_map/ppermute | solution.py:38
  7.8 0.4 collective-permute-start.5
  8.2 0.9 %collective-permute-start = (f32[320,128]{1,0:T(8,128)S(1)}, f32[320,128]{1,0:T(8,128)S(1)}, u32[]{:S(2)}, u32[]{:S(2)}) collective-permute-start(f32[320,128]{1,0:T(8,128)S(1)} %get-tuple-element.24), channel_id=1, source_target_pairs={{0,16},{16,0},{32,48},{48,32},{64,80},{80,64},{96,112},{112,96},{1... | collective-permute-start | bytes 491528 | tf_op jit(solution)/shard_map/ppermute | solution.py:38
  9.1 1.5 %first.1._.moved = f32[3,256,512]{2,1,0:T(8,128)S(1)} custom-call(f32[256,512]{1,0:T(8,128)S(1)} %copy-done, f32[256,512]{1,0:T(8,128)S(1)} %copy-done.1, f32[256,512]{1,0:T(8,128)S(1)} %copy-done.2), custom_call_target="tpu_custom_call" | custom-call | tf_op jit(solution)/shard_map/first/pallas_call | solution.py:546
  10.6 4.5 %collective-permute-done.4.gotfar_a = f32[16,128]{1,0:T(8,128)S(1)} collective-permute-done((f32[16,128]{1,0:T(8,128)S(1)}, f32[16,128]{1,0:T(8,128)S(1)}, u32[]{:S(2)}, u32[]{:S(2)}) %collective-permute-start.4) | collective-permute-done | bytes 8224 | tf_op jit(solution)/shard_map/ppermute | solution.py:38
  15.0 1.3 %collective-permute-start.1 = (f32[320,128]{1,0:T(8,128)S(1)}, f32[320,128]{1,0:T(8,128)S(1)}, u32[]{:S(2)}, u32[]{:S(2)}) collective-permute-start(f32[320,128]{1,0:T(8,128)S(1)} %get-tuple-element.25), channel_id=1, source_target_pairs={{0,240},{16,32},{32,16},{48,64},{64,48},{80,96},{96,80},{112,128},... | collective-permute-start | bytes 491528 | tf_op jit(solution)/shard_map/ppermute | solution.py:38
  16.4 0.0 collective-permute-done.5.gotfar_b
  16.4 0.0 collective-permute-done.2.got_a
  16.4 1.1 %column.1 = (f32[312,128]{1,0:T(8,128)S(1)}, f32[312,128]{1,0:T(8,128)S(1)}, f32[8,128]{1,0:T(8,128)S(1)}, f32[8,128]{1,0:T(8,128)S(1)}, f32[8,128]{1,0:T(8,128)...) custom-call(s32[2]{0:T(128)S(1)} %pad_add_fusion.place, ...), custom_call_target="tpu_custom_call" | custom-call | flops 10000000000 | tf_op jit(solution)/shard_map/column/pallas_call | solution.py:546
  17.6 1.3 %collective-permute-start.6 = (f32[312,128]{1,0:T(8,128)S(1)}, f32[312,128]{1,0:T(8,128)S(1)}, u32[]{:S(2)}, u32[]{:S(2)}) collective-permute-start(f32[312,128]{1,0:T(8,128)S(1)} %get-tuple-element.31), channel_id=1, source_target_pairs={{0,1},{1,0},{2,3},{3,2},{4,5},{5,4},{6,7},{7,6},{8,9},{9,8},{10,11... | collective-permute-start | bytes 479240 | tf_op jit(solution)/shard_map/ppermute | solution.py:38
  18.8 6.7 %collective-permute-start.7 = (f32[312,128]{1,0:T(8,128)S(1)}, f32[312,128]{1,0:T(8,128)S(1)}, u32[]{:S(2)}, u32[]{:S(2)}) collective-permute-start(f32[312,128]{1,0:T(8,128)S(1)} %get-tuple-element.32), channel_id=1, source_target_pairs={{0,15},{1,2},{2,1},{3,4},{4,3},{5,6},{6,5},{7,8},{8,7},{9,10},{10,... | collective-permute-start | bytes 479240 | tf_op jit(solution)/shard_map/ppermute | solution.py:38
  25.5 0.0 collective-permute-start.8
  25.5 0.0 collective-permute-done.mid_a
  25.5 3.9 %collective-permute-start.9 = (f32[8,128]{1,0:T(8,128)S(1)}, f32[8,128]{1,0:T(8,128)S(1)}, u32[]{:S(2)}, u32[]{:S(2)}) collective-permute-start(f32[8,128]{1,0:T(8,128)S(1)} %get-tuple-element.36), channel_id=1, source_target_pairs={{0,14},{1,15},{2,4},{3,5},{4,2},{5,3},{6,8},{7,9},{8,6},{9,7},{10,... | collective-permute-start | bytes 12296 | tf_op jit(solution)/shard_map/ppermute | solution.py:38
  29.4 5.0 %collective-permute-done.7.got_b = f32[312,128]{1,0:T(8,128)S(1)} collective-permute-done((f32[312,128]{1,0:T(8,128)S(1)}, f32[312,128]{1,0:T(8,128)S(1)}, u32[]{:S(2)}, u32[]{:S(2)}) %collective-permute-start.7) | collective-permute-done | bytes 159776 | tf_op jit(solution)/shard_map/ppermute | solution.py:38
  34.4 6.4 %main.1 = (f32[256,512]{1,0:T(8,128)S(1)}, f32[256,512]{1,0:T(8,128)S(1)}, f32[256,512]{1,0:T(8,128)S(1)}, f32[256,128]{1,0:T(8,128)S(1)}) custom-call(s32[2]{0:T(128)S(1)} %pad_add_fusion.place, f32[3,264,128]{2,1,0:T(8,128)S(1)} %get-tuple-element.23.own, f32[320,128]{1,0:T(8,128)S(1)} %collective-permute-done.mid_a, ...), custom_call_target="tpu_custom_call" | custom-call | flops 10000000000 | tf_op jit(solution)/shard_map/main/pallas_call | solution.py:546
  40.9 3.5 %strip.1 = (f32[256,512]{1,0:T(8,128)}, f32[256,512]{1,0:T(8,128)}, f32[256,512]{1,0:T(8,128)}) custom-call(s32[2]{0:T(128)S(1)} %pad_add_fusion.place, f32[256,128]{1,0:T(8,128)S(1)} %get-tuple-element.33.total, f32[8,128]{1,0:T(8,128)S(1)} %get-tuple-element.34.tail1, f32[312,128]{1,0:T(8,128)S(1)} %collective-permute-done.6.got_a, ...), custom_call_target="tpu_custom_call" | custom-call | tf_op jit(solution)/shard_map/strip/pallas_call | solution.py:546
  (10 shorter events, 0.0 us)
Async XLA Ops:
  0.6 8.4 %copy-start.2 = (f32[256,512]{1,0:T(8,128)S(1)}, f32[256,512]{1,0:T(8,128)}, u32[]{:S(2)}) copy-start(f32[256,512]{1,0:T(8,128)} %n_b.1) | copy-start | bytes 1572868
  0.6 8.4 %copy-start.1 = (f32[256,512]{1,0:T(8,128)S(1)}, f32[256,512]{1,0:T(8,128)}, u32[]{:S(2)}) copy-start(f32[256,512]{1,0:T(8,128)} %m_b.1) | copy-start | bytes 1572868
  0.7 8.4 %copy-start = (f32[256,512]{1,0:T(8,128)S(1)}, f32[256,512]{1,0:T(8,128)}, u32[]{:S(2)}) copy-start(f32[256,512]{1,0:T(8,128)} %h_b.1) | copy-start | bytes 1572868
  0.7 15.6 %copy-start.3 = (s32[256,512]{1,0:T(8,128)S(1)}, s32[256,512]{1,0:T(8,128)}, u32[]{:S(2)}) copy-start(s32[256,512]{1,0:T(8,128)} %w_b.1) | copy-start | bytes 1572868
  4.2 12.2 %collective-permute-start.2 = (f32[600,128]{1,0:T(8,128)S(1)}, f32[600,128]{1,0:T(8,128)S(1)}, u32[]{:S(2)}, u32[]{:S(2)}) collective-permute-start(f32[600,128]{1,0:T(8,128)S(1)} %get-tuple-element.27), channel_id=1, source_target_pairs={{0,16},{16,0},{32,48},{48,32},{64,80},{80,64},{96,112},{112,96},{1... | collective-permute-start | bytes 921608 | tf_op jit(solution)/shard_map/ppermute | solution.py:38
  4.9 11.5 %collective-permute-start.3 = (f32[600,128]{1,0:T(8,128)S(1)}, f32[600,128]{1,0:T(8,128)S(1)}, u32[]{:S(2)}, u32[]{:S(2)}) collective-permute-start(f32[600,128]{1,0:T(8,128)S(1)} %get-tuple-element.28), channel_id=1, source_target_pairs={{0,240},{16,32},{32,16},{48,64},{64,48},{80,96},{96,80},{112,128},... | collective-permute-start | bytes 921608 | tf_op jit(solution)/shard_map/ppermute | solution.py:38
  6.5 8.5 %collective-permute-start.4 = (f32[16,128]{1,0:T(8,128)S(1)}, f32[16,128]{1,0:T(8,128)S(1)}, u32[]{:S(2)}, u32[]{:S(2)}) collective-permute-start(f32[16,128]{1,0:T(8,128)S(1)} %get-tuple-element.29), channel_id=1, source_target_pairs={{0,32},{16,48},{32,0},{48,16},{64,96},{80,112},{96,64},{112,80},{1... | collective-permute-start | bytes 24584 | tf_op jit(solution)/shard_map/ppermute | solution.py:38
  7.8 8.6 %collective-permute-start.5 = (f32[16,128]{1,0:T(8,128)S(1)}, f32[16,128]{1,0:T(8,128)S(1)}, u32[]{:S(2)}, u32[]{:S(2)}) collective-permute-start(f32[16,128]{1,0:T(8,128)S(1)} %get-tuple-element.30), channel_id=1, source_target_pairs={{0,224},{16,240},{32,64},{48,80},{64,32},{80,48},{96,128},{112,144... | collective-permute-start | bytes 24584 | tf_op jit(solution)/shard_map/ppermute | solution.py:38
  8.2 17.3 %collective-permute-start = (f32[320,128]{1,0:T(8,128)S(1)}, f32[320,128]{1,0:T(8,128)S(1)}, u32[]{:S(2)}, u32[]{:S(2)}) collective-permute-start(f32[320,128]{1,0:T(8,128)S(1)} %get-tuple-element.24), channel_id=1, source_target_pairs={{0,16},{16,0},{32,48},{48,32},{64,80},{80,64},{96,112},{112,96},{1... | collective-permute-start | bytes 491528 | tf_op jit(solution)/shard_map/ppermute | solution.py:38
  15.0 14.3 %collective-permute-start.1 = (f32[320,128]{1,0:T(8,128)S(1)}, f32[320,128]{1,0:T(8,128)S(1)}, u32[]{:S(2)}, u32[]{:S(2)}) collective-permute-start(f32[320,128]{1,0:T(8,128)S(1)} %get-tuple-element.25), channel_id=1, source_target_pairs={{0,240},{16,32},{32,16},{48,64},{64,48},{80,96},{96,80},{112,128},... | collective-permute-start | bytes 491528 | tf_op jit(solution)/shard_map/ppermute | solution.py:38
  17.6 11.8 %collective-permute-start.6 = (f32[312,128]{1,0:T(8,128)S(1)}, f32[312,128]{1,0:T(8,128)S(1)}, u32[]{:S(2)}, u32[]{:S(2)}) collective-permute-start(f32[312,128]{1,0:T(8,128)S(1)} %get-tuple-element.31), channel_id=1, source_target_pairs={{0,1},{1,0},{2,3},{3,2},{4,5},{5,4},{6,7},{7,6},{8,9},{9,8},{10,11... | collective-permute-start | bytes 479240 | tf_op jit(solution)/shard_map/ppermute | solution.py:38
  18.8 15.6 %collective-permute-start.7 = (f32[312,128]{1,0:T(8,128)S(1)}, f32[312,128]{1,0:T(8,128)S(1)}, u32[]{:S(2)}, u32[]{:S(2)}) collective-permute-start(f32[312,128]{1,0:T(8,128)S(1)} %get-tuple-element.32), channel_id=1, source_target_pairs={{0,15},{1,2},{2,1},{3,4},{4,3},{5,6},{6,5},{7,8},{8,7},{9,10},{10,... | collective-permute-start | bytes 479240 | tf_op jit(solution)/shard_map/ppermute | solution.py:38
  25.5 15.4 %collective-permute-start.8 = (f32[8,128]{1,0:T(8,128)S(1)}, f32[8,128]{1,0:T(8,128)S(1)}, u32[]{:S(2)}, u32[]{:S(2)}) collective-permute-start(f32[8,128]{1,0:T(8,128)S(1)} %get-tuple-element.35), channel_id=1, source_target_pairs={{0,2},{1,3},{2,0},{3,1},{4,6},{5,7},{6,4},{7,5},{8,10},{9,11},{10,... | collective-permute-start | bytes 12296 | tf_op jit(solution)/shard_map/ppermute | solution.py:38
  25.5 15.4 %collective-permute-start.9 = (f32[8,128]{1,0:T(8,128)S(1)}, f32[8,128]{1,0:T(8,128)S(1)}, u32[]{:S(2)}, u32[]{:S(2)}) collective-permute-start(f32[8,128]{1,0:T(8,128)S(1)} %get-tuple-element.36), channel_id=1, source_target_pairs={{0,14},{1,15},{2,4},{3,5},{4,2},{5,3},{6,8},{7,9},{8,6},{9,7},{10,... | collective-permute-start | bytes 12296 | tf_op jit(solution)/shard_map/ppermute | solution.py:38

commit v2 on v1

--- a/solution.py
+++ b/solution.py
@@ -23,8 +23,8 @@
 COL_MSG = RING + 48
 MID_MSG = COL_MSG + 8
 TALL = 3 * LANES
-UNROLL = 4
-VMEM_LIMIT = 48 * 1024 * 1024
+UNROLL = 8
+VMEM_LIMIT = 24 * 1024 * 1024
 
 
 def partners(axis, parity, reach):
@@ -161,7 +161,7 @@
 
 
 def column_kernel(
-    place, _, own, rim, got_a, got_b, gotfar_a, gotfar_b, h_l, h_r, m_l, m_r, n_l, n_r, w_l, w_r,
+    place, own, rim, got_a, got_b, gotfar_a, gotfar_b, h_in, m_in, n_in, w_in,
     msg_a, msg_b, far_a, far_b, tail1, ring, turned_own, edges, lanes,
 ):
     i, j = place[0], place[1]
@@ -217,14 +217,16 @@
         moved = pltpu.roll(block, (target - source) % LANES, 1) if target != source else block
         return jnp.where((lane >= target) & (lane < target + count), moved, packed)
 
-    fields = ((h_l, h_r), (m_l, m_r), (n_l, n_r), (w_l, w_r))
+    fields = (h_in, m_in, n_in, w_in)
     lane = lax.broadcasted_iota(jnp.int32, (ROWS, LANES), 1)
     packed = jnp.zeros((ROWS, LANES), jnp.float32)
     lane8 = lax.broadcasted_iota(jnp.int32, (8, LANES), 1)
     packed8 = jnp.zeros((8, LANES), jnp.float32)
-    for f, (left, right) in enumerate(fields):
-        packed = tuck(packed, lane, right[...].astype(jnp.float32), LANES - 8, 8 * f, 8)
-        packed = tuck(packed, lane, left[...].astype(jnp.float32), 0, 32 + 8 * f, 8)
+    for f, field in enumerate(fields):
+        right = field[:, COLS - LANES : COLS].astype(jnp.float32)
+        packed = tuck(packed, lane, right, LANES - 8, 8 * f, 8)
+        left = field[:, 0:LANES].astype(jnp.float32)
+        packed = tuck(packed, lane, left, 0, 32 + 8 * f, 8)
         packed8 = tuck(packed8, lane8, edges[f, :, COLS - LANES : COLS], LANES - 8, 8 * f, 8)
         packed8 = tuck(packed8, lane8, edges[f, :, 0:LANES], 0, 32 + 8 * f, 8)
     spots = ((2, LANES - 1, 64), (0, 0, 65), (0, LANES - 1, 66), (2, 0, 67))
@@ -275,11 +277,9 @@
 
 def widen(value, spread):
     part = value.astype(jnp.bfloat16)
-    rest = value - part.astype(jnp.float32)
-    part2 = rest.astype(jnp.bfloat16)
-    part3 = (rest - part2.astype(jnp.float32)).astype(jnp.bfloat16)
+    rest = (value - part.astype(jnp.float32)).astype(jnp.bfloat16)
     dot = functools.partial(jnp.dot, preferred_element_type=jnp.float32)
-    return dot(part, spread) + dot(part2, spread) + dot(part3, spread)
+    return dot(part, spread) + dot(rest, spread)
 
 
 def fluxes(height, east, north):
@@ -295,7 +295,7 @@
     return quarter, (fm, fmm, fmn), (gn, fmn, gnn)
 
 
-def interior_step(load, store):
+def interior_step(load, store, ready=None):
     sub = lax.broadcasted_iota(jnp.int32, (8, COLS), 0)
     first_row, last_row = sub == 0, sub == 7
     zeros = jnp.zeros((8, COLS), jnp.float32)
@@ -319,19 +319,44 @@
         finish(pl.multiple_of(jnp.maximum(c - 1, 0) * 8, 8), partial, ahead)
         return new_partial, below
 
-    partial, _ = lax.fori_loop(0, ROWS // 8, body, ([zeros] * 3, [zeros] * 3), unroll=UNROLL)
-    finish(ROWS - 8, partial, [zeros] * 3)
-
-
-def first_kernel(h_in, m_in, n_in, moved):
+    carry = ([zeros] * 3, [zeros] * 3)
+    if ready is None:
+        carry = lax.fori_loop(0, ROWS // 8, body, carry, unroll=UNROLL)
+    else:
+        for q in range(4):
+            ready(q)
+            carry = lax.fori_loop(q * 8, q * 8 + 8, body, carry, unroll=UNROLL)
+    finish(ROWS - 8, carry[0], [zeros] * 3)
+
+
+def first_kernel(h_in, m_in, n_in, w_in, h_near, m_near, n_near, w_near, moved, sems):
+    part = ROWS // 4
+    pairs = ((h_in, h_near), (m_in, m_near), (n_in, n_near))
+
+    def fetch(pair, q, sem):
+        rows = slice(q * part, q * part + part)
+        return pltpu.make_async_copy(pair[0].at[rows], pair[1].at[rows], sem)
+
+    copies = [[fetch(pair, q, sems.at[q, f]) for f, pair in enumerate(pairs)] for q in range(4)]
+    mask = pltpu.make_async_copy(w_in, w_near, sems.at[4, 0])
+    for q in range(4):
+        for copy in copies[q]:
+            copy.start()
+    mask.start()
+
     def load(at):
-        return [ref[pl.ds(at, 8), :] for ref in (h_in, m_in, n_in)]
+        return [ref[pl.ds(at, 8), :] for ref in (h_near, m_near, n_near)]
 
     def store(at, values):
         for f in range(3):
             moved[f, pl.ds(at, 8), :] = values[f]
 
-    interior_step(load, store)
+    def ready(q):
+        for copy in copies[q]:
+            copy.wait()
+
+    interior_step(load, store, ready)
+    mask.wait()
 
 
 def main_kernel(
@@ -383,9 +408,17 @@
 
 def strip_kernel(
     place, total, tail1, got_a, got_b, gotfar_a, gotfar_b, ring, turned_own, edges,
-    h_t, h_b, m_t, m_b, n_t, n_b, w_t, w_b, h_in, m_in, n_in,
-    h_out, m_out, n_out, block,
+    h_0, m_0, n_0, w_in, h_in, m_in, n_in, h_out, m_out, n_out, block, sides, ends, sems,
 ):
+    inner = slice(LANES, COLS - LANES)
+    copies = []
+    for f, (source, target) in enumerate(((h_in, h_out), (m_in, m_out), (n_in, n_out))):
+        rows = slice(8, ROWS - 8)
+        copies.append(
+            pltpu.make_async_copy(source.at[rows, inner], target.at[rows, inner], sems.at[0, f])
+        )
+        copies[f].start()
+
     i, j = place[0], place[1]
     even_j = j % 2 == 0
     even2_j = (j // 2) % 2 == 0
@@ -414,13 +447,13 @@
         six([fine[6 * s + r : 6 * s + r + 1] for r in range(6)]) for s in range(STEPS)
     ]
     row_state = []
-    for f, (top, bottom) in enumerate(((h_t, h_b), (m_t, m_b), (n_t, n_b), (w_t, w_b))):
+    for f, field in enumerate((h_0, m_0, n_0, w_in)):
         row_state.append(
             jnp.concatenate(
                 [
                     edges[f, 4:8, :],
-                    top[...].astype(jnp.float32),
-                    bottom[...].astype(jnp.float32),
+                    field[0:8, :].astype(jnp.float32),
+                    field[ROWS - 8 : ROWS, :].astype(jnp.float32),
                     edges[f, 0:4, :],
                 ],
                 axis=0,
@@ -486,8 +519,12 @@
             value = jnp.where((sub == 3) & ends[0], pltpu.roll(value, n_sub - 1, 0), value)
             value = jnp.where((sub == 20) & ends[1], pltpu.roll(value, 1, 0), value)
             if len(ends) == 4:
-                value = jnp.where((lanes == n_lane - 1) & ends[2], pltpu.roll(value, n_lane - 1, 1), value)
-                value = jnp.where((lanes == ROWS) & ends[3], pltpu.roll(value, 1, 1), value)
+                blocks = [value[:, k * LANES : (k + 1) * LANES] for k in range(3)]
+                last = lanes[:, 0:LANES] == LANES - 1
+                blocks[2] = jnp.where(last & ends[2], pltpu.roll(blocks[0], LANES - 1, 1), blocks[2])
+                initial = lanes[:, 0:LANES] == 0
+                blocks[2] = jnp.where(initial & ends[3], pltpu.roll(blocks[1], 1, 1), blocks[2])
+                value = jnp.concatenate(blocks, axis=1)
             fixed.append(value)
         quarter, east_flux, north_flux = fluxes(*fixed)
         along_sub, along_lane = (east_flux, north_flux) if x_axis == 0 else (north_flux, east_flux)
@@ -508,7 +545,7 @@
         cols = advance(cols, col_lift[s], col_state[3], 1, col_ends)
 
     lane = lax.broadcasted_iota(jnp.int32, (ROWS, LANES), 1)
-    for f, (source, target) in enumerate(((h_in, h_out), (m_in, m_out), (n_in, n_out))):
+    for f in range(3):
         block[8 * f : 8 * f + 4, :] = cols[f][16:20, 0:LANES]
         block[8 * f + 4 : 8 * f + 8, :] = cols[f][4:8, 0:LANES]
     upper = block[...].T
@@ -517,37 +554,45 @@
         block[8 * f + 4 : 8 * f + 8, :] = cols[f][4:8, LANES : 2 * LANES]
     rim = jnp.concatenate([upper, block[...].T], axis=0)
     for f, (source, target) in enumerate(((h_in, h_out), (m_in, m_out), (n_in, n_out))):
-        value = jnp.concatenate(
-            [rows[f][4:8], source[4 : ROWS - 4, :], rows[f][16:20]], axis=0
-        )
         side = pltpu.roll(rim, (LANES - 4 - 8 * f) % LANES, 1)
-        target[:, 0:LANES] = jnp.where(lane < 4, side, value[:, 0:LANES])
-        target[:, LANES : COLS - LANES] = value[:, LANES : COLS - LANES]
-        target[:, COLS - LANES : COLS] = jnp.where(
-            lane >= LANES - 4, side, value[:, COLS - LANES : COLS]
-        )
-
-
-def whole(shape):
-    return pl.BlockSpec(shape, lambda g: (0,) * len(shape))
-
-
-def smem():
-    return pl.BlockSpec(memory_space=pltpu.SMEM)
+        top = jnp.concatenate([rows[f][4:8], source[4:8, :]], axis=0)
+        bottom = jnp.concatenate([source[ROWS - 8 : ROWS - 4, :], rows[f][16:20]], axis=0)
+        for t, (at, mine) in enumerate(((0, lane < 4), (COLS - LANES, lane >= LANES - 4))):
+            part = slice(at, at + LANES)
+            value = jnp.concatenate(
+                [top[:, part], source[8 : ROWS - 8, part], bottom[:, part]], axis=0
+            )
+            sides[f, t] = jnp.where(mine, side, value)
+            copies.append(
+                pltpu.make_async_copy(sides.at[f, t], target.at[:, part], sems.at[1 + t, f])
+            )
+        for t, (at, value) in enumerate(((0, top), (ROWS - 8, bottom))):
+            ends[f, t] = value[:, inner]
+            copies.append(
+                pltpu.make_async_copy(ends.at[f, t], target.at[at : at + 8, inner], sems.at[3 + t, f])
+            )
+        for copy in copies[-4:]:
+            copy.start()
+    for copy in copies:
+        copy.wait()
 
 
 def f32(*shape):
     return jax.ShapeDtypeStruct(shape, jnp.float32)
 
 
-def run(body, outs, in_specs, scratch, args, name, cost=None):
+SMEM = pl.BlockSpec(memory_space=pltpu.SMEM)
+VMEM = pl.BlockSpec(memory_space=pltpu.VMEM)
+HBM = pl.BlockSpec(memory_space=pltpu.HBM)
+
+
+def run(body, outs, in_specs, scratch, args, name, cost=None, out_spec=VMEM):
     if cost is not None:
         cost = pl.CostEstimate(flops=cost, bytes_accessed=0, transcendentals=0)
     return pl.pallas_call(
         body,
-        grid=(1,),
         in_specs=in_specs,
-        out_specs=[whole(o.shape) for o in outs],
+        out_specs=[out_spec] * len(outs),
         out_shape=outs,
         scratch_shapes=scratch,
         compiler_params=pltpu.CompilerParams(vmem_limit_bytes=VMEM_LIMIT),
@@ -559,14 +604,12 @@
 def shards(slip_rate, green_kernel, intersection, wet_mask, column_height, east_flow, north_flow):
     place = jnp.stack([lax.axis_index("ox"), lax.axis_index("oy")]).astype(jnp.int32)
     fields = (column_height, east_flow, north_flow, wet_mask)
-    twice = tuple(x for x in fields for _ in range(2))
-
-    far_away = pl.BlockSpec(memory_space=pltpu.HBM)
+
     msg_a, msg_b, mid_a, mid_b, far_a, far_b, own, rim = run(
         slip_kernel,
         [f32(ROW_MSG, LANES)] * 2 + [f32(MID_MSG, LANES)] * 2 + [f32(16, LANES)] * 2
         + [f32(3, RING, LANES), f32(8, LANES)],
-        [smem()] + [far_away] * 7,
+        [SMEM] + [HBM] * 7,
         [
             pltpu.VMEM((9, 32, UX * LANES), jnp.bfloat16),
             pltpu.SMEM((1, 9), jnp.int32),
@@ -590,24 +633,23 @@
     mid_a = swap(mid_a, "ox", 0)
     mid_b = swap(mid_b, "ox", 1)
 
-    side = [
-        pl.BlockSpec((ROWS, LANES), lambda g: (0, 0)),
-        pl.BlockSpec((ROWS, LANES), lambda g: (0, COLS // LANES - 1)),
-    ]
-    tile = whole((ROWS, COLS))
-    (moved,) = run(
-        first_kernel, [f32(3, ROWS, COLS)], [tile] * 3, [], fields[:3], "first", None
+    *near, moved = run(
+        first_kernel,
+        [f32(ROWS, COLS)] * 3 + [jax.ShapeDtypeStruct((ROWS, COLS), jnp.int32), f32(3, ROWS, COLS)],
+        [HBM] * 4,
+        [pltpu.SemaphoreType.DMA((5, 3))],
+        [pltpu.with_memory_space_constraint(x, pltpu.HBM) for x in fields],
+        "first",
     )
+    near = tuple(near)
     msg_a, msg_b, far_a, far_b, tail1, ring, turned_own, edges = run(
         column_kernel,
         [f32(COL_MSG, LANES)] * 2 + [f32(8, LANES)] * 4 + [f32(3, 64, LANES), f32(4, 8, COLS)],
-        [smem(), pl.BlockSpec(memory_space=pl.ANY), whole((3, RING, LANES)), whole((8, LANES))]
-        + [whole((ROW_MSG, LANES))] * 2
-        + [whole((16, LANES))] * 2 + side * 4,
+        [SMEM] + [VMEM] * 10,
         [pltpu.VMEM((TALL, LANES), jnp.float32)],
-        (place, moved, own, rim, got_a, got_b, gotfar_a, gotfar_b) + twice,
+        (place, own, rim, got_a, got_b, gotfar_a, gotfar_b) + near,
         "column",
-        10000000000,
+        10**10,
     )
     got_a = swap(msg_a, "oy", 0)
     got_b = swap(msg_b, "oy", 1)
@@ -617,31 +659,30 @@
     height, east, north, total = run(
         main_kernel,
         [f32(ROWS, COLS)] * 3 + [f32(MAIN, LANES)],
-        [smem(), whole((3, RING, LANES))] + [whole((MID_MSG, LANES))] * 2
-        + [whole((COL_MSG, LANES))] * 2 + [whole((3, ROWS, COLS)), tile],
+        [SMEM] + [VMEM] * 7,
         [
             pltpu.VMEM((2, 3, ROWS, COLS), jnp.float32),
             pltpu.VMEM((MAIN, COLS), jnp.float32),
         ],
-        (place, own, mid_a, mid_b, got_a, got_b, moved, wet_mask),
+        (place, own, mid_a, mid_b, got_a, got_b, moved, near[3]),
         "main",
-        10000000000,
+        10**10,
     )
-    ends = [
-        pl.BlockSpec((8, COLS), lambda g: (0, 0)),
-        pl.BlockSpec((8, COLS), lambda g: (ROWS // 8 - 1, 0)),
-    ]
     return tuple(
         run(
             strip_kernel,
             [f32(ROWS, COLS)] * 3,
-            [smem(), whole((MAIN, LANES)), whole((8, LANES))] + [whole((COL_MSG, LANES))] * 2
-            + [whole((8, LANES))] * 3 + [whole((3, 64, LANES)), whole((4, 8, COLS))] + ends * 4
-            + [tile] * 3,
-            [pltpu.VMEM((LANES, LANES), jnp.float32)],
+            [SMEM] + [VMEM] * 16,
+            [
+                pltpu.VMEM((LANES, LANES), jnp.float32),
+                pltpu.VMEM((3, 2, ROWS, LANES), jnp.float32),
+                pltpu.VMEM((3, 2, 8, COLS - 2 * LANES), jnp.float32),
+                pltpu.SemaphoreType.DMA((5, 3)),
+            ],
             (place, total, tail1, got_a, got_b, gotfar_a, gotfar_b, ring, turned_own, edges)
-            + twice + (height, east, north),
+            + near + (height, east, north),
             "strip",
+            out_spec=HBM,
         )
     )
 

time: 44.5 us -> 43.5 us (0.978)
  waiting for transfers between devices: 9.51 us -> 8.39 us
    ppermute x10, waiting for transfers between devices: 9.51 us -> 8.39 us  [swap(): return lax.ppermute(value, axis, partners(axis, parity, reach))]
  transfers between devices with their start and end apart: 10 -> 10, of which waited for: 2 -> 2; matrix products, arithmetic and copies ran while one was open for 0% -> 0% of each run, Pallas kernels for 21% -> 23%
where the time goes in v2:
time: 43.5 us; the launch traced here: 43.4 us
  starting transfers between devices  18 us (41%)
  Pallas kernels  16.2 us (37%)
  waiting for transfers between devices  8.39 us (19%)
  between operations  0.69 us (2%)
    ppermute x10, starting transfers between devices, swap(): return lax.ppermute(value, axis, partners(axis, parity, reach))  18 us
    pallas_call x5, Pallas kernels, run(): pl.pallas_call(body, in_specs=in_specs, out_specs=[out_spec] * len(outs),...  16.2 us
    ppermute x10, waiting for transfers between devices, swap(): return lax.ppermute(value, axis, partners(axis, parity, reach))  8.39 us
  transfers between devices with their start and end apart: 10, of which 2 were waited for; matrix products, arithmetic and copies ran while one was open for 0% of the time, Pallas kernels for 23%

profile of v2, /device:TPU:25, one launch (start us, length us, event | category | flops | bytes accessed | tf_op | source)
XLA Modules:
  0.0 43.4 jit_solution(3475917675723576114)
XLA Ops:
  0.6 0.1 pad_add_fusion.place
  0.7 3.4 %slip.1 = (f32[600,128]{1,0:T(8,128)S(1)}, f32[600,128]{1,0:T(8,128)S(1)}, f32[320,128]{1,0:T(8,128)S(1)}, f32[320,128]{1,0:T(8,128)S(1)}, f32[16,128]{1,0:T(8,1...) custom-call(s32[2]{0:T(128)S(1)} %pad_add_fusion.place, s32[1,9]{1,0:T(1,128)} %cover_in.1, ...), custom_call_target="tpu_custom_call" | custom-call | tf_op jit(solution)/shard_map/slip/pallas_call | solution.py:592
  4.1 0.8 %collective-permute-start.2 = (f32[600,128]{1,0:T(8,128)S(1)}, f32[600,128]{1,0:T(8,128)S(1)}, u32[]{:S(2)}, u32[]{:S(2)}) collective-permute-start(f32[600,128]{1,0:T(8,128)S(1)} %get-tuple-element.32), channel_id=1, source_target_pairs={{0,16},{16,0},{32,48},{48,32},{64,80},{80,64},{96,112},{112,96},{1... | collective-permute-start | bytes 921608 | tf_op jit(solution)/shard_map/ppermute | solution.py:38
  4.9 1.6 %collective-permute-start.3 = (f32[600,128]{1,0:T(8,128)S(1)}, f32[600,128]{1,0:T(8,128)S(1)}, u32[]{:S(2)}, u32[]{:S(2)}) collective-permute-start(f32[600,128]{1,0:T(8,128)S(1)} %get-tuple-element.33), channel_id=1, source_target_pairs={{0,240},{16,32},{32,16},{48,64},{64,48},{80,96},{96,80},{112,128},... | collective-permute-start | bytes 921608 | tf_op jit(solution)/shard_map/ppermute | solution.py:38
  6.5 1.2 %collective-permute-start.4 = (f32[16,128]{1,0:T(8,128)S(1)}, f32[16,128]{1,0:T(8,128)S(1)}, u32[]{:S(2)}, u32[]{:S(2)}) collective-permute-start(f32[16,128]{1,0:T(8,128)S(1)} %get-tuple-element.34), channel_id=1, source_target_pairs={{0,32},{16,48},{32,0},{48,16},{64,96},{80,112},{96,64},{112,80},{1... | collective-permute-start | bytes 24584 | tf_op jit(solution)/shard_map/ppermute | solution.py:38
  7.7 0.4 collective-permute-start.5
  8.2 0.9 %collective-permute-start = (f32[320,128]{1,0:T(8,128)S(1)}, f32[320,128]{1,0:T(8,128)S(1)}, u32[]{:S(2)}, u32[]{:S(2)}) collective-permute-start(f32[320,128]{1,0:T(8,128)S(1)} %get-tuple-element.29), channel_id=1, source_target_pairs={{0,16},{16,0},{32,48},{48,32},{64,80},{80,64},{96,112},{112,96},{1... | collective-permute-start | bytes 491528 | tf_op jit(solution)/shard_map/ppermute | solution.py:38
  9.0 2.7 %first.1 = (f32[256,512]{1,0:T(8,128)S(1)}, f32[256,512]{1,0:T(8,128)S(1)}, f32[256,512]{1,0:T(8,128)S(1)}, s32[256,512]{1,0:T(8,128)S(1)}, f32[3,256,512]{2,1,0:T(8,128)S(1)}) custom-call(f32[256,512]{1,0:T(8,128)} %h_in.3, f32[256,512]{1,0:T(8,128)} %m_in.3, f32[256,512]{1,0:T(8,128)} %n_in.3, s32[256,512]{1,0:T(8,128)} %w_in.3), custom_call_target="tpu_custom_call" | custom-call | tf_op jit(solution)/shard_map/first/pallas_call | solution.py:592
  11.7 3.3 %collective-permute-done.4.gotfar_a = f32[16,128]{1,0:T(8,128)S(1)} collective-permute-done((f32[16,128]{1,0:T(8,128)S(1)}, f32[16,128]{1,0:T(8,128)S(1)}, u32[]{:S(2)}, u32[]{:S(2)}) %collective-permute-start.4) | collective-permute-done | bytes 8224 | tf_op jit(solution)/shard_map/ppermute | solution.py:38
  15.0 1.3 %collective-permute-start.1 = (f32[320,128]{1,0:T(8,128)S(1)}, f32[320,128]{1,0:T(8,128)S(1)}, u32[]{:S(2)}, u32[]{:S(2)}) collective-permute-start(f32[320,128]{1,0:T(8,128)S(1)} %get-tuple-element.30), channel_id=1, source_target_pairs={{0,240},{16,32},{32,16},{48,64},{64,48},{80,96},{96,80},{112,128},... | collective-permute-start | bytes 491528 | tf_op jit(solution)/shard_map/ppermute | solution.py:38
  16.3 0.0 collective-permute-done.5.gotfar_b
  16.3 0.0 collective-permute-done.2.got_a
  16.3 0.0 collective-permute-done.3.got_b
  16.4 1.1 %column.1 = (f32[312,128]{1,0:T(8,128)S(1)}, f32[312,128]{1,0:T(8,128)S(1)}, f32[8,128]{1,0:T(8,128)S(1)}, f32[8,128]{1,0:T(8,128)S(1)}, f32[8,128]{1,0:T(8,128)...) custom-call(s32[2]{0:T(128)S(1)} %pad_add_fusion.place, ...), custom_call_target="tpu_custom_call" | custom-call | flops 10000000000 | tf_op jit(solution)/shard_map/column/pallas_call | solution.py:592
  17.5 1.3 %collective-permute-start.6 = (f32[312,128]{1,0:T(8,128)S(1)}, f32[312,128]{1,0:T(8,128)S(1)}, u32[]{:S(2)}, u32[]{:S(2)}) collective-permute-start(f32[312,128]{1,0:T(8,128)S(1)} %get-tuple-element.40), channel_id=1, source_target_pairs={{0,1},{1,0},{2,3},{3,2},{4,5},{5,4},{6,7},{7,6},{8,9},{9,8},{10,11... | collective-permute-start | bytes 479240 | tf_op jit(solution)/shard_map/ppermute | solution.py:38
  18.8 6.7 %collective-permute-start.7 = (f32[312,128]{1,0:T(8,128)S(1)}, f32[312,128]{1,0:T(8,128)S(1)}, u32[]{:S(2)}, u32[]{:S(2)}) collective-permute-start(f32[312,128]{1,0:T(8,128)S(1)} %get-tuple-element.41), channel_id=1, source_target_pairs={{0,15},{1,2},{2,1},{3,4},{4,3},{5,6},{6,5},{7,8},{8,7},{9,10},{10,... | collective-permute-start | bytes 479240 | tf_op jit(solution)/shard_map/ppermute | solution.py:38
  25.5 0.0 collective-permute-start.8
  25.5 0.0 collective-permute-done.mid_a
  25.5 3.9 %collective-permute-start.9 = (f32[8,128]{1,0:T(8,128)S(1)}, f32[8,128]{1,0:T(8,128)S(1)}, u32[]{:S(2)}, u32[]{:S(2)}) collective-permute-start(f32[8,128]{1,0:T(8,128)S(1)} %get-tuple-element.46), channel_id=1, source_target_pairs={{0,14},{1,15},{2,4},{3,5},{4,2},{5,3},{6,8},{7,9},{8,6},{9,7},{10,... | collective-permute-start | bytes 12296 | tf_op jit(solution)/shard_map/ppermute | solution.py:38
  29.3 0.0 collective-permute-done.1.mid_b
  29.3 5.1 %collective-permute-done.7.got_b = f32[312,128]{1,0:T(8,128)S(1)} collective-permute-done((f32[312,128]{1,0:T(8,128)S(1)}, f32[312,128]{1,0:T(8,128)S(1)}, u32[]{:S(2)}, u32[]{:S(2)}) %collective-permute-start.7) | collective-permute-done | bytes 159776 | tf_op jit(solution)/shard_map/ppermute | solution.py:38
  34.4 6.0 %main.1 = (f32[256,512]{1,0:T(8,128)S(1)}, f32[256,512]{1,0:T(8,128)S(1)}, f32[256,512]{1,0:T(8,128)S(1)}, f32[256,128]{1,0:T(8,128)S(1)}) custom-call(s32[2]{0:T(128)S(1)} %pad_add_fusion.place, f32[3,264,128]{2,1,0:T(8,128)S(1)} %get-tuple-element.28.own, f32[320,128]{1,0:T(8,128)S(1)} %collective-permute-done.mid_a, ...), custom_call_target="tpu_custom_call" | custom-call | flops 10000000000 | tf_op jit(solution)/shard_map/main/pallas_call | solution.py:592
  40.4 0.0 collective-permute-done.9.gotfar_b
  40.5 2.9 %strip.1 = (f32[256,512]{1,0:T(8,128)}, f32[256,512]{1,0:T(8,128)}, f32[256,512]{1,0:T(8,128)}) custom-call(s32[2]{0:T(128)S(1)} %pad_add_fusion.place, f32[256,128]{1,0:T(8,128)S(1)} %get-tuple-element.43.total, f32[8,128]{1,0:T(8,128)S(1)} %get-tuple-element.44.tail1, f32[312,128]{1,0:T(8,128)S(1)} %collective-permute-done.6.got_a, ...), custom_call_target="tpu_custom_call" | custom-call | tf_op jit(solution)/shard_map/strip/pallas_call | solution.py:592
  (2 shorter events, 0.0 us)
Async XLA Ops:
  4.1 12.2 %collective-permute-start.2 = (f32[600,128]{1,0:T(8,128)S(1)}, f32[600,128]{1,0:T(8,128)S(1)}, u32[]{:S(2)}, u32[]{:S(2)}) collective-permute-start(f32[600,128]{1,0:T(8,128)S(1)} %get-tuple-element.32), channel_id=1, source_target_pairs={{0,16},{16,0},{32,48},{48,32},{64,80},{80,64},{96,112},{112,96},{1... | collective-permute-start | bytes 921608 | tf_op jit(solution)/shard_map/ppermute | solution.py:38
  4.9 11.5 %collective-permute-start.3 = (f32[600,128]{1,0:T(8,128)S(1)}, f32[600,128]{1,0:T(8,128)S(1)}, u32[]{:S(2)}, u32[]{:S(2)}) collective-permute-start(f32[600,128]{1,0:T(8,128)S(1)} %get-tuple-element.33), channel_id=1, source_target_pairs={{0,240},{16,32},{32,16},{48,64},{64,48},{80,96},{96,80},{112,128},... | collective-permute-start | bytes 921608 | tf_op jit(solution)/shard_map/ppermute | solution.py:38
  6.5 8.5 %collective-permute-start.4 = (f32[16,128]{1,0:T(8,128)S(1)}, f32[16,128]{1,0:T(8,128)S(1)}, u32[]{:S(2)}, u32[]{:S(2)}) collective-permute-start(f32[16,128]{1,0:T(8,128)S(1)} %get-tuple-element.34), channel_id=1, source_target_pairs={{0,32},{16,48},{32,0},{48,16},{64,96},{80,112},{96,64},{112,80},{1... | collective-permute-start | bytes 24584 | tf_op jit(solution)/shard_map/ppermute | solution.py:38
  7.7 8.6 %collective-permute-start.5 = (f32[16,128]{1,0:T(8,128)S(1)}, f32[16,128]{1,0:T(8,128)S(1)}, u32[]{:S(2)}, u32[]{:S(2)}) collective-permute-start(f32[16,128]{1,0:T(8,128)S(1)} %get-tuple-element.35), channel_id=1, source_target_pairs={{0,224},{16,240},{32,64},{48,80},{64,32},{80,48},{96,128},{112,144... | collective-permute-start | bytes 24584 | tf_op jit(solution)/shard_map/ppermute | solution.py:38
  8.2 17.3 %collective-permute-start = (f32[320,128]{1,0:T(8,128)S(1)}, f32[320,128]{1,0:T(8,128)S(1)}, u32[]{:S(2)}, u32[]{:S(2)}) collective-permute-start(f32[320,128]{1,0:T(8,128)S(1)} %get-tuple-element.29), channel_id=1, source_target_pairs={{0,16},{16,0},{32,48},{48,32},{64,80},{80,64},{96,112},{112,96},{1... | collective-permute-start | bytes 491528 | tf_op jit(solution)/shard_map/ppermute | solution.py:38
  15.0 14.3 %collective-permute-start.1 = (f32[320,128]{1,0:T(8,128)S(1)}, f32[320,128]{1,0:T(8,128)S(1)}, u32[]{:S(2)}, u32[]{:S(2)}) collective-permute-start(f32[320,128]{1,0:T(8,128)S(1)} %get-tuple-element.30), channel_id=1, source_target_pairs={{0,240},{16,32},{32,16},{48,64},{64,48},{80,96},{96,80},{112,128},... | collective-permute-start | bytes 491528 | tf_op jit(solution)/shard_map/ppermute | solution.py:38
  17.5 11.8 %collective-permute-start.6 = (f32[312,128]{1,0:T(8,128)S(1)}, f32[312,128]{1,0:T(8,128)S(1)}, u32[]{:S(2)}, u32[]{:S(2)}) collective-permute-start(f32[312,128]{1,0:T(8,128)S(1)} %get-tuple-element.40), channel_id=1, source_target_pairs={{0,1},{1,0},{2,3},{3,2},{4,5},{5,4},{6,7},{7,6},{8,9},{9,8},{10,11... | collective-permute-start | bytes 479240 | tf_op jit(solution)/shard_map/ppermute | solution.py:38
  18.8 15.6 %collective-permute-start.7 = (f32[312,128]{1,0:T(8,128)S(1)}, f32[312,128]{1,0:T(8,128)S(1)}, u32[]{:S(2)}, u32[]{:S(2)}) collective-permute-start(f32[312,128]{1,0:T(8,128)S(1)} %get-tuple-element.41), channel_id=1, source_target_pairs={{0,15},{1,2},{2,1},{3,4},{4,3},{5,6},{6,5},{7,8},{8,7},{9,10},{10,... | collective-permute-start | bytes 479240 | tf_op jit(solution)/shard_map/ppermute | solution.py:38
  25.5 15.0 %collective-permute-start.8 = (f32[8,128]{1,0:T(8,128)S(1)}, f32[8,128]{1,0:T(8,128)S(1)}, u32[]{:S(2)}, u32[]{:S(2)}) collective-permute-start(f32[8,128]{1,0:T(8,128)S(1)} %get-tuple-element.45), channel_id=1, source_target_pairs={{0,2},{1,3},{2,0},{3,1},{4,6},{5,7},{6,4},{7,5},{8,10},{9,11},{10,... | collective-permute-start | bytes 12296 | tf_op jit(solution)/shard_map/ppermute | solution.py:38
  25.5 15.0 %collective-permute-start.9 = (f32[8,128]{1,0:T(8,128)S(1)}, f32[8,128]{1,0:T(8,128)S(1)}, u32[]{:S(2)}, u32[]{:S(2)}) collective-permute-start(f32[8,128]{1,0:T(8,128)S(1)} %get-tuple-element.46), channel_id=1, source_target_pairs={{0,14},{1,15},{2,4},{3,5},{4,2},{5,3},{6,8},{7,9},{8,6},{9,7},{10,... | collective-permute-start | bytes 12296 | tf_op jit(solution)/shard_map/ppermute | solution.py:38

commit v3 on v2

--- a/solution.py
+++ b/solution.py
@@ -23,7 +23,7 @@
 COL_MSG = RING + 48
 MID_MSG = COL_MSG + 8
 TALL = 3 * LANES
-UNROLL = 8
+UNROLL = 16
 VMEM_LIMIT = 24 * 1024 * 1024
 
 
@@ -300,11 +300,11 @@
     first_row, last_row = sub == 0, sub == 7
     zeros = jnp.zeros((8, COLS), jnp.float32)
 
-    def finish(at, partial, ahead):
-        store(at, [p + jnp.where(last_row, u, 0.0) for p, u in zip(partial, ahead)])
+    def finish(at, partial, ahead, beyond):
+        store(at, [p + jnp.where(last_row, b, a) for p, a, b in zip(partial, ahead, beyond)])
 
     def body(c, carry):
-        partial, above = carry
+        partial, above, before = carry
         at = pl.multiple_of(c * 8, 8)
         quarter, east_flux, north_flux = fluxes(*load(at))
         below = [pltpu.roll(q + x, 1, 0) for q, x in zip(quarter, east_flux)]
@@ -313,20 +313,19 @@
             pltpu.roll(q - g, COLS - 1, 1)
             + pltpu.roll(q + g, 1, 1)
             + jnp.where(first_row, a, b)
-            + jnp.where(last_row, 0.0, u)
-            for q, g, a, b, u in zip(quarter, north_flux, above, below, ahead)
+            for q, g, a, b in zip(quarter, north_flux, above, below)
         ]
-        finish(pl.multiple_of(jnp.maximum(c - 1, 0) * 8, 8), partial, ahead)
-        return new_partial, below
-
-    carry = ([zeros] * 3, [zeros] * 3)
+        finish(pl.multiple_of(jnp.maximum(c - 1, 0) * 8, 8), partial, before, ahead)
+        return new_partial, below, ahead
+
+    carry = ([zeros] * 3, [zeros] * 3, [zeros] * 3)
     if ready is None:
         carry = lax.fori_loop(0, ROWS // 8, body, carry, unroll=UNROLL)
     else:
         for q in range(4):
             ready(q)
-            carry = lax.fori_loop(q * 8, q * 8 + 8, body, carry, unroll=UNROLL)
-    finish(ROWS - 8, carry[0], [zeros] * 3)
+            carry = lax.fori_loop(q * 8, q * 8 + 8, body, carry, unroll=8)
+    finish(ROWS - 8, carry[0], carry[2], carry[2])
 
 
 def first_kernel(h_in, m_in, n_in, w_in, h_near, m_near, n_near, w_near, moved, sems):

time: 43.5 us -> 43.5 us (level)
  transfers between devices with their start and end apart: 10 -> 10, of which waited for: 2 -> 2; matrix products, arithmetic and copies ran while one was open for 0% -> 0% of each run, Pallas kernels for 23% -> 22%
where the time goes in v3:
time: 43.5 us; the launch traced here: 43.4 us
  starting transfers between devices  18 us (41%)
  Pallas kernels  15.9 us (37%)
  waiting for transfers between devices  8.44 us (19%)
  between operations  0.85 us (2%)
    ppermute x10, starting transfers between devices, swap(): return lax.ppermute(value, axis, partners(axis, parity, reach))  18 us
    pallas_call x5, Pallas kernels, run(): pl.pallas_call(body, in_specs=in_specs, out_specs=[out_spec] * len(outs),...  15.9 us
    ppermute x10, waiting for transfers between devices, swap(): return lax.ppermute(value, axis, partners(axis, parity, reach))  8.44 us
  transfers between devices with their start and end apart: 10, of which 2 were waited for; matrix products, arithmetic and copies ran while one was open for 0% of the time, Pallas kernels for 22%

profile of v3, /device:TPU:25, one launch (start us, length us, event | category | flops | bytes accessed | tf_op | source)
XLA Modules:
  0.0 43.4 jit_solution(13530574190396731435)
XLA Ops:
  0.6 0.1 pad_add_fusion.place
  0.7 3.4 %slip.1 = (f32[600,128]{1,0:T(8,128)S(1)}, f32[600,128]{1,0:T(8,128)S(1)}, f32[320,128]{1,0:T(8,128)S(1)}, f32[320,128]{1,0:T(8,128)S(1)}, f32[16,128]{1,0:T(8,1...) custom-call(s32[2]{0:T(128)S(1)} %pad_add_fusion.place, s32[1,9]{1,0:T(1,128)} %cover_in.1, ...), custom_call_target="tpu_custom_call" | custom-call | tf_op jit(solution)/shard_map/slip/pallas_call | solution.py:591
  4.1 0.8 %collective-permute-start.2 = (f32[600,128]{1,0:T(8,128)S(1)}, f32[600,128]{1,0:T(8,128)S(1)}, u32[]{:S(2)}, u32[]{:S(2)}) collective-permute-start(f32[600,128]{1,0:T(8,128)S(1)} %get-tuple-element.32), channel_id=1, source_target_pairs={{0,16},{16,0},{32,48},{48,32},{64,80},{80,64},{96,112},{112,96},{1... | collective-permute-start | bytes 921608 | tf_op jit(solution)/shard_map/ppermute | solution.py:38
  4.9 1.6 %collective-permute-start.3 = (f32[600,128]{1,0:T(8,128)S(1)}, f32[600,128]{1,0:T(8,128)S(1)}, u32[]{:S(2)}, u32[]{:S(2)}) collective-permute-start(f32[600,128]{1,0:T(8,128)S(1)} %get-tuple-element.33), channel_id=1, source_target_pairs={{0,240},{16,32},{32,16},{48,64},{64,48},{80,96},{96,80},{112,128},... | collective-permute-start | bytes 921608 | tf_op jit(solution)/shard_map/ppermute | solution.py:38
  6.5 1.2 %collective-permute-start.4 = (f32[16,128]{1,0:T(8,128)S(1)}, f32[16,128]{1,0:T(8,128)S(1)}, u32[]{:S(2)}, u32[]{:S(2)}) collective-permute-start(f32[16,128]{1,0:T(8,128)S(1)} %get-tuple-element.34), channel_id=1, source_target_pairs={{0,32},{16,48},{32,0},{48,16},{64,96},{80,112},{96,64},{112,80},{1... | collective-permute-start | bytes 24584 | tf_op jit(solution)/shard_map/ppermute | solution.py:38
  7.7 0.4 collective-permute-start.5
  8.2 0.9 %collective-permute-start = (f32[320,128]{1,0:T(8,128)S(1)}, f32[320,128]{1,0:T(8,128)S(1)}, u32[]{:S(2)}, u32[]{:S(2)}) collective-permute-start(f32[320,128]{1,0:T(8,128)S(1)} %get-tuple-element.29), channel_id=1, source_target_pairs={{0,16},{16,0},{32,48},{48,32},{64,80},{80,64},{96,112},{112,96},{1... | collective-permute-start | bytes 491528 | tf_op jit(solution)/shard_map/ppermute | solution.py:38
  9.0 2.6 %first.1 = (f32[256,512]{1,0:T(8,128)S(1)}, f32[256,512]{1,0:T(8,128)S(1)}, f32[256,512]{1,0:T(8,128)S(1)}, s32[256,512]{1,0:T(8,128)S(1)}, f32[3,256,512]{2,1,0:T(8,128)S(1)}) custom-call(f32[256,512]{1,0:T(8,128)} %h_in.3, f32[256,512]{1,0:T(8,128)} %m_in.3, f32[256,512]{1,0:T(8,128)} %n_in.3, s32[256,512]{1,0:T(8,128)} %w_in.3), custom_call_target="tpu_custom_call" | custom-call | tf_op jit(solution)/shard_map/first/pallas_call | solution.py:591
  11.6 3.4 %collective-permute-done.4.gotfar_a = f32[16,128]{1,0:T(8,128)S(1)} collective-permute-done((f32[16,128]{1,0:T(8,128)S(1)}, f32[16,128]{1,0:T(8,128)S(1)}, u32[]{:S(2)}, u32[]{:S(2)}) %collective-permute-start.4) | collective-permute-done | bytes 8224 | tf_op jit(solution)/shard_map/ppermute | solution.py:38
  15.0 1.3 %collective-permute-start.1 = (f32[320,128]{1,0:T(8,128)S(1)}, f32[320,128]{1,0:T(8,128)S(1)}, u32[]{:S(2)}, u32[]{:S(2)}) collective-permute-start(f32[320,128]{1,0:T(8,128)S(1)} %get-tuple-element.30), channel_id=1, source_target_pairs={{0,240},{16,32},{32,16},{48,64},{64,48},{80,96},{96,80},{112,128},... | collective-permute-start | bytes 491528 | tf_op jit(solution)/shard_map/ppermute | solution.py:38
  16.3 0.0 collective-permute-done.5.gotfar_b
  16.3 0.0 collective-permute-done.2.got_a
  16.3 0.0 collective-permute-done.3.got_b
  16.4 1.1 %column.1 = (f32[312,128]{1,0:T(8,128)S(1)}, f32[312,128]{1,0:T(8,128)S(1)}, f32[8,128]{1,0:T(8,128)S(1)}, f32[8,128]{1,0:T(8,128)S(1)}, f32[8,128]{1,0:T(8,128)...) custom-call(s32[2]{0:T(128)S(1)} %pad_add_fusion.place, ...), custom_call_target="tpu_custom_call" | custom-call | flops 10000000000 | tf_op jit(solution)/shard_map/column/pallas_call | solution.py:591
  17.5 1.3 %collective-permute-start.6 = (f32[312,128]{1,0:T(8,128)S(1)}, f32[312,128]{1,0:T(8,128)S(1)}, u32[]{:S(2)}, u32[]{:S(2)}) collective-permute-start(f32[312,128]{1,0:T(8,128)S(1)} %get-tuple-element.40), channel_id=1, source_target_pairs={{0,1},{1,0},{2,3},{3,2},{4,5},{5,4},{6,7},{7,6},{8,9},{9,8},{10,11... | collective-permute-start | bytes 479240 | tf_op jit(solution)/shard_map/ppermute | solution.py:38
  18.8 6.7 %collective-permute-start.7 = (f32[312,128]{1,0:T(8,128)S(1)}, f32[312,128]{1,0:T(8,128)S(1)}, u32[]{:S(2)}, u32[]{:S(2)}) collective-permute-start(f32[312,128]{1,0:T(8,128)S(1)} %get-tuple-element.41), channel_id=1, source_target_pairs={{0,15},{1,2},{2,1},{3,4},{4,3},{5,6},{6,5},{7,8},{8,7},{9,10},{10,... | collective-permute-start | bytes 479240 | tf_op jit(solution)/shard_map/ppermute | solution.py:38
  25.5 0.0 collective-permute-start.8
  25.5 3.9 %collective-permute-start.9 = (f32[8,128]{1,0:T(8,128)S(1)}, f32[8,128]{1,0:T(8,128)S(1)}, u32[]{:S(2)}, u32[]{:S(2)}) collective-permute-start(f32[8,128]{1,0:T(8,128)S(1)} %get-tuple-element.46), channel_id=1, source_target_pairs={{0,14},{1,15},{2,4},{3,5},{4,2},{5,3},{6,8},{7,9},{8,6},{9,7},{10,... | collective-permute-start | bytes 12296 | tf_op jit(solution)/shard_map/ppermute | solution.py:38
  29.3 0.0 collective-permute-done.1.mid_b
  29.3 0.0 collective-permute-done.6.got_a
  29.3 5.0 %collective-permute-done.7.got_b = f32[312,128]{1,0:T(8,128)S(1)} collective-permute-done((f32[312,128]{1,0:T(8,128)S(1)}, f32[312,128]{1,0:T(8,128)S(1)}, u32[]{:S(2)}, u32[]{:S(2)}) %collective-permute-start.7) | collective-permute-done | bytes 159776 | tf_op jit(solution)/shard_map/ppermute | solution.py:38
  34.4 5.9 %main.1 = (f32[256,512]{1,0:T(8,128)S(1)}, f32[256,512]{1,0:T(8,128)S(1)}, f32[256,512]{1,0:T(8,128)S(1)}, f32[256,128]{1,0:T(8,128)S(1)}) custom-call(s32[2]{0:T(128)S(1)} %pad_add_fusion.place, f32[3,264,128]{2,1,0:T(8,128)S(1)} %get-tuple-element.28.own, f32[320,128]{1,0:T(8,128)S(1)} %collective-permute-done.mid_a, ...), custom_call_target="tpu_custom_call" | custom-call | flops 10000000000 | tf_op jit(solution)/shard_map/main/pallas_call | solution.py:591
  40.3 0.0 collective-permute-done.9.gotfar_b
  40.3 2.9 %strip.1 = (f32[256,512]{1,0:T(8,128)}, f32[256,512]{1,0:T(8,128)}, f32[256,512]{1,0:T(8,128)}) custom-call(s32[2]{0:T(128)S(1)} %pad_add_fusion.place, f32[256,128]{1,0:T(8,128)S(1)} %get-tuple-element.43.total, f32[8,128]{1,0:T(8,128)S(1)} %get-tuple-element.44.tail1, f32[312,128]{1,0:T(8,128)S(1)} %collective-permute-done.6.got_a, ...), custom_call_target="tpu_custom_call" | custom-call | tf_op jit(solution)/shard_map/strip/pallas_call | solution.py:591
  (2 shorter events, 0.0 us)
Async XLA Ops:
  4.1 12.2 %collective-permute-start.2 = (f32[600,128]{1,0:T(8,128)S(1)}, f32[600,128]{1,0:T(8,128)S(1)}, u32[]{:S(2)}, u32[]{:S(2)}) collective-permute-start(f32[600,128]{1,0:T(8,128)S(1)} %get-tuple-element.32), channel_id=1, source_target_pairs={{0,16},{16,0},{32,48},{48,32},{64,80},{80,64},{96,112},{112,96},{1... | collective-permute-start | bytes 921608 | tf_op jit(solution)/shard_map/ppermute | solution.py:38
  4.9 11.5 %collective-permute-start.3 = (f32[600,128]{1,0:T(8,128)S(1)}, f32[600,128]{1,0:T(8,128)S(1)}, u32[]{:S(2)}, u32[]{:S(2)}) collective-permute-start(f32[600,128]{1,0:T(8,128)S(1)} %get-tuple-element.33), channel_id=1, source_target_pairs={{0,240},{16,32},{32,16},{48,64},{64,48},{80,96},{96,80},{112,128},... | collective-permute-start | bytes 921608 | tf_op jit(solution)/shard_map/ppermute | solution.py:38
  6.5 8.5 %collective-permute-start.4 = (f32[16,128]{1,0:T(8,128)S(1)}, f32[16,128]{1,0:T(8,128)S(1)}, u32[]{:S(2)}, u32[]{:S(2)}) collective-permute-start(f32[16,128]{1,0:T(8,128)S(1)} %get-tuple-element.34), channel_id=1, source_target_pairs={{0,32},{16,48},{32,0},{48,16},{64,96},{80,112},{96,64},{112,80},{1... | collective-permute-start | bytes 24584 | tf_op jit(solution)/shard_map/ppermute | solution.py:38
  7.7 8.6 %collective-permute-start.5 = (f32[16,128]{1,0:T(8,128)S(1)}, f32[16,128]{1,0:T(8,128)S(1)}, u32[]{:S(2)}, u32[]{:S(2)}) collective-permute-start(f32[16,128]{1,0:T(8,128)S(1)} %get-tuple-element.35), channel_id=1, source_target_pairs={{0,224},{16,240},{32,64},{48,80},{64,32},{80,48},{96,128},{112,144... | collective-permute-start | bytes 24584 | tf_op jit(solution)/shard_map/ppermute | solution.py:38
  8.2 17.3 %collective-permute-start = (f32[320,128]{1,0:T(8,128)S(1)}, f32[320,128]{1,0:T(8,128)S(1)}, u32[]{:S(2)}, u32[]{:S(2)}) collective-permute-start(f32[320,128]{1,0:T(8,128)S(1)} %get-tuple-element.29), channel_id=1, source_target_pairs={{0,16},{16,0},{32,48},{48,32},{64,80},{80,64},{96,112},{112,96},{1... | collective-permute-start | bytes 491528 | tf_op jit(solution)/shard_map/ppermute | solution.py:38
  15.0 14.3 %collective-permute-start.1 = (f32[320,128]{1,0:T(8,128)S(1)}, f32[320,128]{1,0:T(8,128)S(1)}, u32[]{:S(2)}, u32[]{:S(2)}) collective-permute-start(f32[320,128]{1,0:T(8,128)S(1)} %get-tuple-element.30), channel_id=1, source_target_pairs={{0,240},{16,32},{32,16},{48,64},{64,48},{80,96},{96,80},{112,128},... | collective-permute-start | bytes 491528 | tf_op jit(solution)/shard_map/ppermute | solution.py:38
  17.5 11.8 %collective-permute-start.6 = (f32[312,128]{1,0:T(8,128)S(1)}, f32[312,128]{1,0:T(8,128)S(1)}, u32[]{:S(2)}, u32[]{:S(2)}) collective-permute-start(f32[312,128]{1,0:T(8,128)S(1)} %get-tuple-element.40), channel_id=1, source_target_pairs={{0,1},{1,0},{2,3},{3,2},{4,5},{5,4},{6,7},{7,6},{8,9},{9,8},{10,11... | collective-permute-start | bytes 479240 | tf_op jit(solution)/shard_map/ppermute | solution.py:38
  18.8 15.6 %collective-permute-start.7 = (f32[312,128]{1,0:T(8,128)S(1)}, f32[312,128]{1,0:T(8,128)S(1)}, u32[]{:S(2)}, u32[]{:S(2)}) collective-permute-start(f32[312,128]{1,0:T(8,128)S(1)} %get-tuple-element.41), channel_id=1, source_target_pairs={{0,15},{1,2},{2,1},{3,4},{4,3},{5,6},{6,5},{7,8},{8,7},{9,10},{10,... | collective-permute-start | bytes 479240 | tf_op jit(solution)/shard_map/ppermute | solution.py:38
  25.5 14.8 %collective-permute-start.8 = (f32[8,128]{1,0:T(8,128)S(1)}, f32[8,128]{1,0:T(8,128)S(1)}, u32[]{:S(2)}, u32[]{:S(2)}) collective-permute-start(f32[8,128]{1,0:T(8,128)S(1)} %get-tuple-element.45), channel_id=1, source_target_pairs={{0,2},{1,3},{2,0},{3,1},{4,6},{5,7},{6,4},{7,5},{8,10},{9,11},{10,... | collective-permute-start | bytes 12296 | tf_op jit(solution)/shard_map/ppermute | solution.py:38
  25.5 14.8 %collective-permute-start.9 = (f32[8,128]{1,0:T(8,128)S(1)}, f32[8,128]{1,0:T(8,128)S(1)}, u32[]{:S(2)}, u32[]{:S(2)}) collective-permute-start(f32[8,128]{1,0:T(8,128)S(1)} %get-tuple-element.46), channel_id=1, source_target_pairs={{0,14},{1,15},{2,4},{3,5},{4,2},{5,3},{6,8},{7,9},{8,6},{9,7},{10,... | collective-permute-start | bytes 12296 | tf_op jit(solution)/shard_map/ppermute | solution.py:38

commit v4 on v3

--- a/solution.py
+++ b/solution.py
@@ -160,8 +160,13 @@
             msg_b[at : at + 4, :] = second[:, k * LANES : (k + 1) * LANES]
 
 
+def tuck(packed, lane, block, source, target, count):
+    moved = pltpu.roll(block, (target - source) % LANES, 1) if target != source else block
+    return jnp.where((lane >= target) & (lane < target + count), moved, packed)
+
+
 def column_kernel(
-    place, own, rim, got_a, got_b, gotfar_a, gotfar_b, h_in, m_in, n_in, w_in,
+    place, own, rim, got_a, got_b, gotfar_a, gotfar_b, rim_state,
     msg_a, msg_b, far_a, far_b, tail1, ring, turned_own, edges, lanes,
 ):
     i, j = place[0], place[1]
@@ -213,20 +218,11 @@
                 [from_below(rows), from_above(rows)], axis=0
             )
 
-    def tuck(packed, lane, block, source, target, count):
-        moved = pltpu.roll(block, (target - source) % LANES, 1) if target != source else block
-        return jnp.where((lane >= target) & (lane < target + count), moved, packed)
-
-    fields = (h_in, m_in, n_in, w_in)
     lane = lax.broadcasted_iota(jnp.int32, (ROWS, LANES), 1)
-    packed = jnp.zeros((ROWS, LANES), jnp.float32)
+    packed = rim_state[...]
     lane8 = lax.broadcasted_iota(jnp.int32, (8, LANES), 1)
     packed8 = jnp.zeros((8, LANES), jnp.float32)
-    for f, field in enumerate(fields):
-        right = field[:, COLS - LANES : COLS].astype(jnp.float32)
-        packed = tuck(packed, lane, right, LANES - 8, 8 * f, 8)
-        left = field[:, 0:LANES].astype(jnp.float32)
-        packed = tuck(packed, lane, left, 0, 32 + 8 * f, 8)
+    for f in range(4):
         packed8 = tuck(packed8, lane8, edges[f, :, COLS - LANES : COLS], LANES - 8, 8 * f, 8)
         packed8 = tuck(packed8, lane8, edges[f, :, 0:LANES], 0, 32 + 8 * f, 8)
     spots = ((2, LANES - 1, 64), (0, 0, 65), (0, LANES - 1, 66), (2, 0, 67))
@@ -328,7 +324,7 @@
     finish(ROWS - 8, carry[0], carry[2], carry[2])
 
 
-def first_kernel(h_in, m_in, n_in, w_in, h_near, m_near, n_near, w_near, moved, sems):
+def first_kernel(h_in, m_in, n_in, w_in, h_near, m_near, n_near, w_near, moved, rim_state, sems):
     part = ROWS // 4
     pairs = ((h_in, h_near), (m_in, m_near), (n_in, n_near))
 
@@ -356,6 +352,14 @@
 
     interior_step(load, store, ready)
     mask.wait()
+    lane = lax.broadcasted_iota(jnp.int32, (ROWS, LANES), 1)
+    packed = jnp.zeros((ROWS, LANES), jnp.float32)
+    for f, field in enumerate((h_near, m_near, n_near, w_near)):
+        right = field[:, COLS - LANES : COLS].astype(jnp.float32)
+        packed = tuck(packed, lane, right, LANES - 8, 8 * f, 8)
+        left = field[:, 0:LANES].astype(jnp.float32)
+        packed = tuck(packed, lane, left, 0, 32 + 8 * f, 8)
+    rim_state[...] = packed
 
 
 def main_kernel(
@@ -632,9 +636,9 @@
     mid_a = swap(mid_a, "ox", 0)
     mid_b = swap(mid_b, "ox", 1)
 
-    *near, moved = run(
+    *near, moved, rim_state = run(
         first_kernel,
-        [f32(ROWS, COLS)] * 3 + [jax.ShapeDtypeStruct((ROWS, COLS), jnp.int32), f32(3, ROWS, COLS)],
+        [f32(ROWS, COLS)] * 3 + [jax.ShapeDtypeStruct((ROWS, COLS), jnp.int32), f32(3, ROWS, COLS), f32(ROWS, LANES)],
         [HBM] * 4,
         [pltpu.SemaphoreType.DMA((5, 3))],
         [pltpu.with_memory_space_constraint(x, pltpu.HBM) for x in fields],
@@ -644,9 +648,9 @@
     msg_a, msg_b, far_a, far_b, tail1, ring, turned_own, edges = run(
         column_kernel,
         [f32(COL_MSG, LANES)] * 2 + [f32(8, LANES)] * 4 + [f32(3, 64, LANES), f32(4, 8, COLS)],
-        [SMEM] + [VMEM] * 10,
+        [SMEM] + [VMEM] * 7,
         [pltpu.VMEM((TALL, LANES), jnp.float32)],
-        (place, own, rim, got_a, got_b, gotfar_a, gotfar_b) + near,
+        (place, own, rim, got_a, got_b, gotfar_a, gotfar_b, rim_state),
         "column",
         10**10,
     )

time: 43.5 us -> 43.5 us (level)
  no operation moved by 1% of the time
where the time goes in v4:
time: 43.5 us; the launch traced here: 43.4 us
  starting transfers between devices  18 us (41%)
  Pallas kernels  16 us (37%)
  waiting for transfers between devices  8.39 us (19%)
  between operations  0.85 us (2%)
    ppermute x10, starting transfers between devices, swap(): return lax.ppermute(value, axis, partners(axis, parity, reach))  18 us
    pallas_call x5, Pallas kernels, run(): pl.pallas_call(body, in_specs=in_specs, out_specs=[out_spec] * len(outs),...  16 us
    ppermute x10, waiting for transfers between devices, swap(): return lax.ppermute(value, axis, partners(axis, parity, reach))  8.39 us
  transfers between devices with their start and end apart: 10, of which 2 were waited for; matrix products, arithmetic and copies ran while one was open for 0% of the time, Pallas kernels for 22%

profile of v4, /device:TPU:25, one launch (start us, length us, event | category | flops | bytes accessed | tf_op | source)
XLA Modules:
  0.0 43.4 jit_solution(10384105465393789177)
XLA Ops:
  0.6 0.1 pad_add_fusion.place
  0.7 3.4 %slip.1 = (f32[600,128]{1,0:T(8,128)S(1)}, f32[600,128]{1,0:T(8,128)S(1)}, f32[320,128]{1,0:T(8,128)S(1)}, f32[320,128]{1,0:T(8,128)S(1)}, f32[16,128]{1,0:T(8,1...) custom-call(s32[2]{0:T(128)S(1)} %pad_add_fusion.place, s32[1,9]{1,0:T(1,128)} %cover_in.1, ...), custom_call_target="tpu_custom_call" | custom-call | tf_op jit(solution)/shard_map/slip/pallas_call | solution.py:595
  4.1 0.8 %collective-permute-start.2 = (f32[600,128]{1,0:T(8,128)S(1)}, f32[600,128]{1,0:T(8,128)S(1)}, u32[]{:S(2)}, u32[]{:S(2)}) collective-permute-start(f32[600,128]{1,0:T(8,128)S(1)} %get-tuple-element.33), channel_id=1, source_target_pairs={{0,16},{16,0},{32,48},{48,32},{64,80},{80,64},{96,112},{112,96},{1... | collective-permute-start | bytes 921608 | tf_op jit(solution)/shard_map/ppermute | solution.py:38
  4.9 1.6 %collective-permute-start.3 = (f32[600,128]{1,0:T(8,128)S(1)}, f32[600,128]{1,0:T(8,128)S(1)}, u32[]{:S(2)}, u32[]{:S(2)}) collective-permute-start(f32[600,128]{1,0:T(8,128)S(1)} %get-tuple-element.34), channel_id=1, source_target_pairs={{0,240},{16,32},{32,16},{48,64},{64,48},{80,96},{96,80},{112,128},... | collective-permute-start | bytes 921608 | tf_op jit(solution)/shard_map/ppermute | solution.py:38
  6.5 1.2 %collective-permute-start.4 = (f32[16,128]{1,0:T(8,128)S(1)}, f32[16,128]{1,0:T(8,128)S(1)}, u32[]{:S(2)}, u32[]{:S(2)}) collective-permute-start(f32[16,128]{1,0:T(8,128)S(1)} %get-tuple-element.35), channel_id=1, source_target_pairs={{0,32},{16,48},{32,0},{48,16},{64,96},{80,112},{96,64},{112,80},{1... | collective-permute-start | bytes 24584 | tf_op jit(solution)/shard_map/ppermute | solution.py:38
  7.7 0.4 collective-permute-start.5
  8.1 0.9 %collective-permute-start = (f32[320,128]{1,0:T(8,128)S(1)}, f32[320,128]{1,0:T(8,128)S(1)}, u32[]{:S(2)}, u32[]{:S(2)}) collective-permute-start(f32[320,128]{1,0:T(8,128)S(1)} %get-tuple-element.30), channel_id=1, source_target_pairs={{0,16},{16,0},{32,48},{48,32},{64,80},{80,64},{96,112},{112,96},{1... | collective-permute-start | bytes 491528 | tf_op jit(solution)/shard_map/ppermute | solution.py:38
  9.0 3.0 %first.1 = (f32[256,512]{1,0:T(8,128)S(1)}, f32[256,512]{1,0:T(8,128)S(1)}, f32[256,512]{1,0:T(8,128)S(1)}, s32[256,512]{1,0:T(8,128)S(1)}, f32[3,256,512]{2,1,0:T(8,128)S(1)}, /*index=5*/f32[256,128]{1,0:T(8,128)S(1)}) custom-call(f32[256,512]{1,0:T(8,128)} %h_in.3, f32[256,512]{1,0:T(8,128)} %m_in.3, f32[256,512]{1,0:T(8,128)} %n_in.3, s32[256,512]{1,0:T(8,128)} %w_in.3), custom_call_target="tpu_custom_call" | custom-call | tf_op jit(solution)/shard_map/first/pallas_call | solution.py:595
  12.0 3.0 %collective-permute-done.4.gotfar_a = f32[16,128]{1,0:T(8,128)S(1)} collective-permute-done((f32[16,128]{1,0:T(8,128)S(1)}, f32[16,128]{1,0:T(8,128)S(1)}, u32[]{:S(2)}, u32[]{:S(2)}) %collective-permute-start.4) | collective-permute-done | bytes 8224 | tf_op jit(solution)/shard_map/ppermute | solution.py:38
  15.0 1.3 %collective-permute-start.1 = (f32[320,128]{1,0:T(8,128)S(1)}, f32[320,128]{1,0:T(8,128)S(1)}, u32[]{:S(2)}, u32[]{:S(2)}) collective-permute-start(f32[320,128]{1,0:T(8,128)S(1)} %get-tuple-element.31), channel_id=1, source_target_pairs={{0,240},{16,32},{32,16},{48,64},{64,48},{80,96},{96,80},{112,128},... | collective-permute-start | bytes 491528 | tf_op jit(solution)/shard_map/ppermute | solution.py:38
  16.3 0.0 collective-permute-done.5.gotfar_b
  16.3 0.0 collective-permute-done.2.got_a
  16.3 0.0 collective-permute-done.3.got_b
  16.4 0.9 %column.1 = (f32[312,128]{1,0:T(8,128)S(1)}, f32[312,128]{1,0:T(8,128)S(1)}, f32[8,128]{1,0:T(8,128)S(1)}, f32[8,128]{1,0:T(8,128)S(1)}, f32[8,128]{1,0:T(8,128)...) custom-call(s32[2]{0:T(128)S(1)} %pad_add_fusion.place, ...), custom_call_target="tpu_custom_call" | custom-call | flops 10000000000 | tf_op jit(solution)/shard_map/column/pallas_call | solution.py:595
  17.2 1.3 %collective-permute-start.6 = (f32[312,128]{1,0:T(8,128)S(1)}, f32[312,128]{1,0:T(8,128)S(1)}, u32[]{:S(2)}, u32[]{:S(2)}) collective-permute-start(f32[312,128]{1,0:T(8,128)S(1)} %get-tuple-element.38), channel_id=1, source_target_pairs={{0,1},{1,0},{2,3},{3,2},{4,5},{5,4},{6,7},{7,6},{8,9},{9,8},{10,11... | collective-permute-start | bytes 479240 | tf_op jit(solution)/shard_map/ppermute | solution.py:38
  18.5 6.7 %collective-permute-start.7 = (f32[312,128]{1,0:T(8,128)S(1)}, f32[312,128]{1,0:T(8,128)S(1)}, u32[]{:S(2)}, u32[]{:S(2)}) collective-permute-start(f32[312,128]{1,0:T(8,128)S(1)} %get-tuple-element.39), channel_id=1, source_target_pairs={{0,15},{1,2},{2,1},{3,4},{4,3},{5,6},{6,5},{7,8},{8,7},{9,10},{10,... | collective-permute-start | bytes 479240 | tf_op jit(solution)/shard_map/ppermute | solution.py:38
  25.2 0.0 collective-permute-start.8
  25.2 0.0 collective-permute-done.mid_a
  25.2 3.9 %collective-permute-start.9 = (f32[8,128]{1,0:T(8,128)S(1)}, f32[8,128]{1,0:T(8,128)S(1)}, u32[]{:S(2)}, u32[]{:S(2)}) collective-permute-start(f32[8,128]{1,0:T(8,128)S(1)} %get-tuple-element.45), channel_id=1, source_target_pairs={{0,14},{1,15},{2,4},{3,5},{4,2},{5,3},{6,8},{7,9},{8,6},{9,7},{10,... | collective-permute-start | bytes 12296 | tf_op jit(solution)/shard_map/ppermute | solution.py:38
  29.1 0.0 collective-permute-done.1.mid_b
  29.1 0.0 collective-permute-done.6.got_a
  29.1 5.3 %collective-permute-done.7.got_b = f32[312,128]{1,0:T(8,128)S(1)} collective-permute-done((f32[312,128]{1,0:T(8,128)S(1)}, f32[312,128]{1,0:T(8,128)S(1)}, u32[]{:S(2)}, u32[]{:S(2)}) %collective-permute-start.7) | collective-permute-done | bytes 159776 | tf_op jit(solution)/shard_map/ppermute | solution.py:38
  34.4 5.9 %main.1 = (f32[256,512]{1,0:T(8,128)S(1)}, f32[256,512]{1,0:T(8,128)S(1)}, f32[256,512]{1,0:T(8,128)S(1)}, f32[256,128]{1,0:T(8,128)S(1)}) custom-call(s32[2]{0:T(128)S(1)} %pad_add_fusion.place, f32[3,264,128]{2,1,0:T(8,128)S(1)} %get-tuple-element.29.own, f32[320,128]{1,0:T(8,128)S(1)} %collective-permute-done.mid_a, ...), custom_call_target="tpu_custom_call" | custom-call | flops 10000000000 | tf_op jit(solution)/shard_map/main/pallas_call | solution.py:595
  40.3 2.9 %strip.1 = (f32[256,512]{1,0:T(8,128)}, f32[256,512]{1,0:T(8,128)}, f32[256,512]{1,0:T(8,128)}) custom-call(s32[2]{0:T(128)S(1)} %pad_add_fusion.place, f32[256,128]{1,0:T(8,128)S(1)} %get-tuple-element.42.total, f32[8,128]{1,0:T(8,128)S(1)} %get-tuple-element.43.tail1, f32[312,128]{1,0:T(8,128)S(1)} %collective-permute-done.6.got_a, ...), custom_call_target="tpu_custom_call" | custom-call | tf_op jit(solution)/shard_map/strip/pallas_call | solution.py:595
  (2 shorter events, 0.0 us)
Async XLA Ops:
  4.1 12.2 %collective-permute-start.2 = (f32[600,128]{1,0:T(8,128)S(1)}, f32[600,128]{1,0:T(8,128)S(1)}, u32[]{:S(2)}, u32[]{:S(2)}) collective-permute-start(f32[600,128]{1,0:T(8,128)S(1)} %get-tuple-element.33), channel_id=1, source_target_pairs={{0,16},{16,0},{32,48},{48,32},{64,80},{80,64},{96,112},{112,96},{1... | collective-permute-start | bytes 921608 | tf_op jit(solution)/shard_map/ppermute | solution.py:38
  4.9 11.5 %collective-permute-start.3 = (f32[600,128]{1,0:T(8,128)S(1)}, f32[600,128]{1,0:T(8,128)S(1)}, u32[]{:S(2)}, u32[]{:S(2)}) collective-permute-start(f32[600,128]{1,0:T(8,128)S(1)} %get-tuple-element.34), channel_id=1, source_target_pairs={{0,240},{16,32},{32,16},{48,64},{64,48},{80,96},{96,80},{112,128},... | collective-permute-start | bytes 921608 | tf_op jit(solution)/shard_map/ppermute | solution.py:38
  6.5 8.5 %collective-permute-start.4 = (f32[16,128]{1,0:T(8,128)S(1)}, f32[16,128]{1,0:T(8,128)S(1)}, u32[]{:S(2)}, u32[]{:S(2)}) collective-permute-start(f32[16,128]{1,0:T(8,128)S(1)} %get-tuple-element.35), channel_id=1, source_target_pairs={{0,32},{16,48},{32,0},{48,16},{64,96},{80,112},{96,64},{112,80},{1... | collective-permute-start | bytes 24584 | tf_op jit(solution)/shard_map/ppermute | solution.py:38
  7.7 8.6 %collective-permute-start.5 = (f32[16,128]{1,0:T(8,128)S(1)}, f32[16,128]{1,0:T(8,128)S(1)}, u32[]{:S(2)}, u32[]{:S(2)}) collective-permute-start(f32[16,128]{1,0:T(8,128)S(1)} %get-tuple-element.36), channel_id=1, source_target_pairs={{0,224},{16,240},{32,64},{48,80},{64,32},{80,48},{96,128},{112,144... | collective-permute-start | bytes 24584 | tf_op jit(solution)/shard_map/ppermute | solution.py:38
  8.1 17.0 %collective-permute-start = (f32[320,128]{1,0:T(8,128)S(1)}, f32[320,128]{1,0:T(8,128)S(1)}, u32[]{:S(2)}, u32[]{:S(2)}) collective-permute-start(f32[320,128]{1,0:T(8,128)S(1)} %get-tuple-element.30), channel_id=1, source_target_pairs={{0,16},{16,0},{32,48},{48,32},{64,80},{80,64},{96,112},{112,96},{1... | collective-permute-start | bytes 491528 | tf_op jit(solution)/shard_map/ppermute | solution.py:38
  15.0 14.1 %collective-permute-start.1 = (f32[320,128]{1,0:T(8,128)S(1)}, f32[320,128]{1,0:T(8,128)S(1)}, u32[]{:S(2)}, u32[]{:S(2)}) collective-permute-start(f32[320,128]{1,0:T(8,128)S(1)} %get-tuple-element.31), channel_id=1, source_target_pairs={{0,240},{16,32},{32,16},{48,64},{64,48},{80,96},{96,80},{112,128},... | collective-permute-start | bytes 491528 | tf_op jit(solution)/shard_map/ppermute | solution.py:38
  17.2 11.8 %collective-permute-start.6 = (f32[312,128]{1,0:T(8,128)S(1)}, f32[312,128]{1,0:T(8,128)S(1)}, u32[]{:S(2)}, u32[]{:S(2)}) collective-permute-start(f32[312,128]{1,0:T(8,128)S(1)} %get-tuple-element.38), channel_id=1, source_target_pairs={{0,1},{1,0},{2,3},{3,2},{4,5},{5,4},{6,7},{7,6},{8,9},{9,8},{10,11... | collective-permute-start | bytes 479240 | tf_op jit(solution)/shard_map/ppermute | solution.py:38
  18.5 15.9 %collective-permute-start.7 = (f32[312,128]{1,0:T(8,128)S(1)}, f32[312,128]{1,0:T(8,128)S(1)}, u32[]{:S(2)}, u32[]{:S(2)}) collective-permute-start(f32[312,128]{1,0:T(8,128)S(1)} %get-tuple-element.39), channel_id=1, source_target_pairs={{0,15},{1,2},{2,1},{3,4},{4,3},{5,6},{6,5},{7,8},{8,7},{9,10},{10,... | collective-permute-start | bytes 479240 | tf_op jit(solution)/shard_map/ppermute | solution.py:38
  25.2 15.1 %collective-permute-start.8 = (f32[8,128]{1,0:T(8,128)S(1)}, f32[8,128]{1,0:T(8,128)S(1)}, u32[]{:S(2)}, u32[]{:S(2)}) collective-permute-start(f32[8,128]{1,0:T(8,128)S(1)} %get-tuple-element.44), channel_id=1, source_target_pairs={{0,2},{1,3},{2,0},{3,1},{4,6},{5,7},{6,4},{7,5},{8,10},{9,11},{10,... | collective-permute-start | bytes 12296 | tf_op jit(solution)/shard_map/ppermute | solution.py:38
  25.2 15.1 %collective-permute-start.9 = (f32[8,128]{1,0:T(8,128)S(1)}, f32[8,128]{1,0:T(8,128)S(1)}, u32[]{:S(2)}, u32[]{:S(2)}) collective-permute-start(f32[8,128]{1,0:T(8,128)S(1)} %get-tuple-element.45), channel_id=1, source_target_pairs={{0,14},{1,15},{2,4},{3,5},{4,2},{5,3},{6,8},{7,9},{8,6},{9,7},{10,... | collective-permute-start | bytes 12296 | tf_op jit(solution)/shard_map/ppermute | solution.py:38
